TPU v7x, 256 devices: a whole 4x4x8 slice. The times are simulated.
256 devices in a mesh: mesh: 32 (over x, y, core), elec: 8 (over z).
Axes of the slice: x: 4, y: 4, z: 8, core: 2. Of those that a mesh axis runs over, the one named last changes fastest.
Arguments:
- rhs: float32 [65536, 1024], P('mesh', 'elec'), may hold values from -18 to 18, as said below
- diagonal: float32 [65536], P('mesh'), may hold values from 1 to 3
- tile_values: bfloat16 [2048, 128, 128], P('mesh'), may hold values from -0.011875 to 0.011875
- tile_rows: int32 [2048], P('mesh'), may hold values from 0 to 15
- tile_offsets: int32 [2048], P('mesh'), may hold values from 0 to 2
- tile_count: int32 [32], P('mesh'), may hold values from 1 to 64, 1280 in all
- node_count: int32 [32], P('mesh'), may hold values from 1 to 2048, 49152 in all
- inc_values: bfloat16 [512, 128, 128], P('mesh'), may hold values from -0.1875 to 0.1875
- inc_rows: int32 [512], P('mesh'), may hold values from 0 to 15
- inc_blocks: int32 [512], P('mesh'), may hold values from 0 to 63
Outputs:
- solution: float32 [65536, 1024], P('mesh', 'elec')
- lead_field: float32 [8192, 1024], P(('mesh', 'elec'))
Inputs may be any that keep to these rules, and one draw needn't show every extreme that they name: `rhs`: Right-hand sides of one partition share a scale.
All inputs are finite; a program needn't handle non-finite values. No bound on the sum of `tile_count` or of `node_count` on one device may be relied on, other than what follows from the above.
Results may differ from a plain program's by a relative error of at most 0.0003.
Values sent between devices are 32-bit elements; how exact they have to be, the bound alone decides.
No kernel may reach another device: no remote copies, remote signals or barrier semaphores. Data moves between devices by JAX's collectives and lax.ppermute only.
A program may use at most 64 MiB of HBM per device.

v0:
```python
import jax
import jax.numpy as jnp
from jax import lax
from jax.sharding import PartitionSpec as P

HB = 2
SRCB_DEV = 2
ITERS = 2


def from_behind(value, axis, steps):
    count = lax.axis_size(axis)
    leading, last = (max(0, -steps), min(count, count - steps))
    return lax.ppermute(value, axis, [(source, source + steps) for source in range(leading, last)])


def gram(left, right):
    return jnp.einsum("ni,nj->ij", left, right, precision=lax.Precision.HIGHEST)


def apply_right(field, matrix):
    return jnp.dot(field, matrix, precision=lax.Precision.HIGHEST)


def solve(gmat, hmat):
    return jax.scipy.linalg.cho_solve((jnp.linalg.cholesky(gmat), True), hmat)


def residual_sum(residual):
    return lax.psum(gram(residual, residual), "mesh")


def body(
    rhs,
    diagonal,
    tile_values,
    tile_rows,
    tile_offsets,
    tile_count,
    node_count,
    inc_values,
    inc_rows,
    inc_blocks,
):
    highest = lax.Precision.HIGHEST
    nodes, width = rhs.shape
    blk = tile_values.shape[1]
    rowb = nodes // blk
    slots = tile_values.shape[0]
    mask = (jnp.arange(nodes) < node_count[0]).astype(jnp.float32)[:, None]
    live = (jnp.arange(slots) < tile_count[0]).astype(jnp.float32)
    coupling = tile_values.astype(jnp.float32)
    targets = tile_rows + tile_offsets
    places = jnp.arange(rowb + HB)[:, None]
    row_hits = (places == tile_rows[None, :]).astype(jnp.float32) * live[None, :]
    col_hits = (places == targets[None, :]).astype(jnp.float32) * live[None, :]
    source = mask * rhs
    solution = jnp.zeros_like(source)
    residual = source
    direction = source
    norm_now = residual_sum(residual)
    for step in range(ITERS):
        blocks = direction.reshape(rowb, blk, width)
        ahead = from_behind(blocks[:HB], "mesh", -1)
        padded = jnp.concatenate([blocks, ahead], 0)
        forward = jnp.einsum("tij,tjc->tic", coupling, padded[targets], precision=highest)
        backward = jnp.einsum("tji,tjc->tic", coupling, blocks[tile_rows], precision=highest)
        summed = jnp.einsum("bt,tic->bic", row_hits, forward, precision=highest)
        summed = summed + jnp.einsum("bt,tic->bic", col_hits, backward, precision=highest)
        behind = from_behind(summed[rowb:], "mesh", 1)
        local = summed[:rowb].at[:HB].add(behind)
        image = mask * (diagonal[:, None] * direction + local.reshape(nodes, width))
        curve = lax.psum(gram(direction, image), "mesh")
        alpha = solve(curve, norm_now)
        solution = solution + apply_right(direction, alpha)
        if step + 1 < ITERS:
            residual = residual - apply_right(image, alpha)
            norm_next = residual_sum(residual)
            beta = solve(norm_now, norm_next)
            direction = residual + apply_right(direction, beta)
            norm_now = norm_next
    sol_rows = solution.reshape(rowb, blk, width)[inc_rows]
    contrib = jnp.einsum(
        "tns,tnc->tsc", inc_values.astype(jnp.float32), sol_rows, precision=highest
    )
    owned = SRCB_DEV * blk
    nblk = owned * lax.axis_size("mesh") // blk
    select = (inc_blocks[None, :] - 0 // blk == jnp.arange(nblk)[:, None]).astype(jnp.float32)
    total = lax.psum(
        jnp.einsum("bt,tsc->bsc", select, contrib, precision=highest).reshape(
            owned * lax.axis_size("mesh"), width
        ),
        "mesh",
    )
    mine = lax.dynamic_slice_in_dim(total, lax.axis_index("mesh") * owned, owned, 0)
    lead = lax.all_to_all(mine, "elec", split_axis=0, concat_axis=1, tiled=True)
    return (solution, lead)


def solution(mesh):
    placed = (
        P("mesh", "elec"),
        P("mesh"),
        P("mesh", None, None),
        P("mesh"),
        P("mesh"),
        P("mesh"),
        P("mesh"),
        P("mesh", None, None),
        P("mesh"),
        P("mesh"),
    )
    return jax.shard_map(
        body,
        mesh=mesh,
        in_specs=placed,
        out_specs=(P("mesh", "elec"), P(("mesh", "elec"), None)),
        check_vma=False,
    )
```

profile of v0, /device:TPU:8, one launch (start us, length us, event | category | flops | bytes accessed | tf_op | source)
XLA Modules:
  0.0 676.3 jit_solution(11981142956728572219)
XLA Ops:
  8.0 1.6 broadcast_multiply_fusion
  9.6 1.9 collective-permute-start
  12.2 0.7 compare_select_fusion.2
  12.9 2.8 gather_fusion.1
  15.7 7.6 %convolution_bitcast_fusion.2 = f32[64,128,128]{1,2,0:T(8,128)} fusion(f32[64,128,128]{2,1,0:T(8,128)} %gather_fusion.1, bf16[64,128,128]{2,1,0:T(8,128)(2,1)S(1)} %copy-done), kind=kOutput, calls=%fused_computation.10 | convolution fusion | flops 1610612736 | bytes 10485760 | tf_op jit(solution)/shard_map/tji,tjc->tic/dot_general | solution.py:67
  23.3 5.6 copy.46
  28.9 1.2 pad_maximum_fusion
  30.1 4.0 gather_fusion
  34.1 7.6 %convolution_bitcast_fusion.3 = f32[64,128,128]{1,2,0:T(8,128)} fusion(f32[64,128,128]{2,1,0:T(8,128)} %gather_fusion, bf16[64,128,128]{2,1,0:T(8,128)(2,1)S(1)} %copy-done), kind=kOutput, calls=%fused_computation.11 | convolution fusion | flops 1610612736 | bytes 10485760 | tf_op jit(solution)/shard_map/tij,tjc->tic/dot_general | solution.py:66
  41.7 5.4 copy.44
  47.2 4.0 fusion.28
  51.2 2.1 convolution_add_fusion.3
  53.4 2.8 collective-permute-start.1
  56.2 2.4 fusion.54
  58.7 1.7 collective-permute-done.1
  61.5 1.0 copy-done.6
  62.4 2.5 fusion.53
  65.0 115.1 %all-reduce.12.cloned.1.call-done = (f32[128,128]{0,1:T(8,128)}, f32[128,128]{0,1:T(8,128)}) async-done(((f32[128,128]{0,1:T(8,128)}, f32[128,128]{0,1:T(8,128)}), (f32[128,128]{0,1:T(8,128)}, f32[128,128]{0,1:T(8,128)})) %all-reduce.12.cloned.1.call-update) | async-done | bytes 131088 | tf_op jit(solution)/shard_map/psum | solution.py:30
  180.1 0.9 copy.51
  181.0 0.9 copy.49
  182.0 0.9 fusion.16
  182.9 11.7 %cholesky.59 = f32[128,128]{1,0:T(8,128)S(1)} custom-call(f32[128,128]{1,0:T(8,128)S(1)} %get-tuple-element.34), custom_call_target="Cholesky" | custom-call | tf_op jit(solution)/shard_map/jit(cholesky)/cholesky | solution.py:26
  195.3 0.7 fusion.4
  195.9 9.8 %custom-call.9 = f32[1,128,128]{1,2,0:T(8,128)S(1)} custom-call(f32[1,128,128]{2,1,0:T(8,128)S(1)} %fusion.4), custom_call_target="InvertDiagBlocksLowerTriangular" | custom-call | tf_op jit(solution)/shard_map/jit(_cho_solve)/triangular_solve | solution.py:26
  205.7 1.1 fusion.19
  207.1 2.2 convolution_subtract_fusion
  209.3 1.0 copy-done.3
  210.3 2.5 fusion.56
  213.3 11.7 %cholesky.70 = f32[128,128]{1,0:T(8,128)S(1)} custom-call(f32[128,128]{1,0:T(8,128)S(1)} %get-tuple-element.33), custom_call_target="Cholesky" | custom-call | tf_op jit(solution)/shard_map/jit(cholesky)/cholesky | solution.py:26
  225.0 0.7 compare_reduce_fusion.1
  226.4 9.8 %custom-call.10 = f32[1,128,128]{1,2,0:T(8,128)S(1)} custom-call(f32[1,128,128]{2,1,0:T(8,128)S(1)} %fusion.5), custom_call_target="InvertDiagBlocksLowerTriangular" | custom-call | tf_op jit(solution)/shard_map/jit(_cho_solve)/triangular_solve | solution.py:26
  236.2 83.3 %all-reduce.6.cloned.1.call-done = f32[128,128]{1,0:T(8,128)} async-done(((f32[128,128]{1,0:T(8,128)}), f32[128,128]{1,0:T(8,128)}) %all-reduce.6.cloned.1.call-update) | async-done | bytes 65552 | tf_op jit(solution)/shard_map/psum | solution.py:30
  319.4 1.1 fusion.14
  320.8 2.2 convolution_add_fusion.1
  323.0 1.0 copy-done.1
  324.0 3.3 collective-permute-start.2
  327.4 4.1 gather_fusion.3
  331.5 7.6 %convolution_bitcast_fusion = f32[64,128,128]{1,2,0:T(8,128)} fusion(f32[64,128,128]{2,1,0:T(8,128)} %gather_fusion.3, bf16[64,128,128]{2,1,0:T(8,128)(2,1)S(1)} %copy-done), kind=kOutput, calls=%fused_computation.8 | convolution fusion | flops 1610612736 | bytes 10485760 | tf_op jit(solution)/shard_map/tji,tjc->tic/dot_general | solution.py:67
  339.1 5.6 copy.55
  344.6 2.4 pad_maximum_fusion.1
  347.1 4.2 gather_fusion.2
  351.2 7.6 %convolution_bitcast_fusion.1 = f32[64,128,128]{1,2,0:T(8,128)} fusion(f32[64,128,128]{2,1,0:T(8,128)} %gather_fusion.2, bf16[64,128,128]{2,1,0:T(8,128)(2,1)S(1)} %copy-done), kind=kOutput, calls=%fused_computation.9 | convolution fusion | flops 1610612736 | bytes 10485760 | tf_op jit(solution)/shard_map/tij,tjc->tic/dot_general | solution.py:66
  358.9 5.4 copy.53
  364.3 4.0 fusion.26
  368.3 2.1 convolution_add_fusion.2
  370.5 2.1 collective-permute-start.3
  372.8 4.2 collective-permute-done.3
  378.1 2.5 fusion.57
  380.9 1.9 fusion.55
  382.8 105.0 %all-reduce.8.cloned.1.call-done = f32[128,128]{0,1:T(8,128)} async-done(((f32[128,128]{0,1:T(8,128)}), f32[128,128]{0,1:T(8,128)}) %all-reduce.8.cloned.1.call-update) | async-done | bytes 65552 | tf_op jit(solution)/shard_map/psum | solution.py:73
  487.8 0.9 copy.58
  488.7 0.9 fusion.11
  489.6 11.7 %cholesky.81 = f32[128,128]{1,0:T(8,128)S(1)} custom-call(f32[128,128]{1,0:T(8,128)S(1)} %fusion.11), custom_call_target="Cholesky" | custom-call | tf_op jit(solution)/shard_map/jit(cholesky)/cholesky | solution.py:26
  502.6 9.8 %custom-call.11 = f32[1,128,128]{1,2,0:T(8,128)S(1)} custom-call(f32[1,128,128]{2,1,0:T(8,128)S(1)} %fusion.6), custom_call_target="InvertDiagBlocksLowerTriangular" | custom-call | tf_op jit(solution)/shard_map/jit(_cho_solve)/triangular_solve | solution.py:26
  513.0 2.5 convolution_add_fusion
  515.5 1.6 gather_fusion.4
  517.1 3.3 convolution_bitcast_fusion.4
  520.4 2.6 copy.60
  523.1 3.1 fusion.34
  526.2 4.4 copy.61
  530.7 121.1 %all-reduce.10.cloned.1.call-done = f32[8192,128]{1,0:T(8,128)} async-done(((f32[8192,128]{1,0:T(8,128)}), f32[8192,128]{1,0:T(8,128)}) %all-reduce.10.cloned.1.call-update) | async-done | bytes 4194320 | tf_op jit(solution)/shard_map/psum | solution.py:89
  651.8 0.9 constant_dynamic-slice_fusion
  652.7 16.1 %all_to_all.19 = f32[8,32,128]{2,1,0:T(8,128)S(1)} all-to-all(f32[8,32,128]{2,1,0:T(8,128)S(1)} %bitcast.124), channel_id=1, replica_groups=mesh['mesh'=32,'elec'=8] {'elec'}, dimensions={0} | all-to-all | bytes 262144 | tf_op jit(solution)/shard_map/all_to_all | solution.py:96
  668.8 0.7 copy_bitcast_fusion
  (78 shorter events, 7.0 us)
Async XLA Ops:
  7.2 8.5 %copy-start = (bf16[64,128,128]{2,1,0:T(8,128)(2,1)S(1)}, bf16[64,128,128]{2,1,0:T(8,128)(2,1)}, u32[]{:S(2)}) copy-start(bf16[64,128,128]{2,1,0:T(8,128)(2,1)} %param.19) | copy-start | bytes 6291460
  7.2 172.9 %all-reduce.12.cloned.1.call-start = ((), (), s32[]{:S(2)}) async-start(), calls=%async_computation.4 | async-start | bytes 262144 | tf_op jit(solution)/shard_map/psum | solution.py:30
  9.6 19.2 %collective-permute-start = (f32[2,128,128]{2,1,0:T(8,128)S(1)}, f32[2,128,128]{2,1,0:T(8,128)S(1)}, u32[]{:S(2)}, u32[]{:S(2)}) collective-permute-start(f32[2,128,128]{2,1,0:T(8,128)S(1)} %bitcast.125), channel_id=1, source_target_pairs={{8,0},{16,8},{24,16},{32,24},{40,32},{48,40},{56,48},{64,56},{72,6... | collective-permute-start | bytes 393224 | tf_op jit(solution)/shard_map/ppermute | solution.py:14
  12.9 38.3 %copy-start.17 = (s32[64]{0:T(128)}, s32[64]{0:T(128)S(1)}, u32[]{:S(2)}) copy-start(s32[64]{0:T(128)S(1)} %get-tuple-element.31) | copy-start | bytes 772
  12.9 2.8 copy-start.14
  23.3 27.9 %copy-start.11 = (f32[64]{0:T(128)}, f32[64]{0:T(128)S(1)}, u32[]{:S(2)}) copy-start(f32[64]{0:T(128)S(1)} %compare_convert_fusion) | copy-start | bytes 772
  28.8 5.3 copy-start.13
  41.7 5.4 copy-start.15
  47.1 4.0 copy-start.4
  53.3 7.5 %copy-start.8 = (f32[2048,128]{1,0:T(8,128)S(1)}, f32[2048,128]{1,0:T(8,128)}, u32[]{:S(2)}) copy-start(f32[2048,128]{1,0:T(8,128)} %param.17) | copy-start | bytes 3145732
  53.4 7.5 %copy-start.10 = (f32[2048]{0:T(1024)S(1)}, f32[2048]{0:T(1024)}, u32[]{:S(2)}) copy-start(f32[2048]{0:T(1024)} %param.18) | copy-start | bytes 24580
  53.4 6.9 %collective-permute-start.1 = (f32[2,128,128]{2,0,1:T(2,128)S(1)}, f32[2,128,128]{2,0,1:T(2,128)S(1)}, u32[]{:S(2)}, u32[]{:S(2)}) collective-permute-start(f32[2,128,128]{2,0,1:T(2,128)S(1)} %slice.109), channel_id=1, source_target_pairs={{0,8},{8,16},{16,24},{24,32},{32,40},{40,48},{48,56},{56,64},{64,7... | collective-permute-start | bytes 393224 | tf_op jit(solution)/shard_map/ppermute | solution.py:14
  61.5 1.0 copy-start.6
  65.0 254.4 %all-reduce.6.cloned.1.call-start = ((), (), s32[]{:S(2)}) async-start(), calls=%async_computation.1 | async-start | bytes 131072 | tf_op jit(solution)/shard_map/psum | solution.py:30
  209.3 1.0 copy-start.3
  212.7 275.1 %all-reduce.8.cloned.1.call-start = ((), (), s32[]{:S(2)}) async-start(), calls=%async_computation.2 | async-start | bytes 131072 | tf_op jit(solution)/shard_map/psum | solution.py:73
  323.0 1.1 copy-start.1
  324.0 20.6 %collective-permute-start.2 = (f32[2,128,128]{2,1,0:T(8,128)S(1)}, f32[2,128,128]{2,1,0:T(8,128)S(1)}, u32[]{:S(2)}, u32[]{:S(2)}) collective-permute-start(f32[2,128,128]{2,1,0:T(8,128)S(1)} %bitcast.126), channel_id=1, source_target_pairs={{8,0},{16,8},{24,16},{32,24},{40,32},{48,40},{56,48},{64,56},{72,6... | collective-permute-start | bytes 393224 | tf_op jit(solution)/shard_map/ppermute | solution.py:14
  358.9 5.4 copy-start.12
  358.9 5.4 copy-start.16
  364.3 4.0 copy-start.5
  364.3 4.0 copy-start.18
  368.3 4.3 copy-start.20
  370.5 6.9 %copy-start.2 = (f32[2048,128]{1,0:T(8,128)S(1)}, f32[2048,128]{1,0:T(8,128)}, u32[]{:S(2)}) copy-start(f32[2048,128]{1,0:T(8,128)} %copy-done.1) | copy-start | bytes 3145732
  370.5 6.4 collective-permute-start.3
  377.4 135.0 %copy-start.9 = (f32[128,128]{1,0:T(8,128)S(1)}, f32[128,128]{1,0:T(8,128)}, u32[]{:S(2)}) copy-start(f32[128,128]{1,0:T(8,128)} %all-reduce.6.cloned.1.call-done) | copy-start | bytes 196612
  380.6 271.2 %all-reduce.10.cloned.1.call-start = ((), (), s32[]{:S(2)}) async-start(), calls=%async_computation.3 | async-start | bytes 8388608 | tf_op jit(solution)/shard_map/psum | solution.py:89
  515.5 10.7 %copy-start.7 = (f32[2048,128]{1,0:T(8,128)}, f32[2048,128]{1,0:T(8,128)S(1)}, u32[]{:S(2)}) copy-start(f32[2048,128]{1,0:T(8,128)S(1)} %convolution_add_fusion) | copy-start | bytes 3145732
  515.5 7.6 %copy-start.19 = (s32[16]{0:T(128)S(1)}, s32[16]{0:T(128)}, u32[]{:S(2)}) copy-start(s32[16]{0:T(128)} %param.26) | copy-start | bytes 196
Sparse Core Ops, SparseCore 0:
  65.1 114.9 all-reduce.11
  212.9 106.5 all-reduce.5
  380.7 107.0 all-reduce.7
  530.8 120.9 all-reduce.9
where the time goes:
time: 683 us; the launch traced here: 676 us
  waiting for transfers between devices  430 us (63%)
  other arithmetic  77.7 us (11%)
  matrix products  71.1 us (10%)
  local copies, waits for them, and re-layouts  54 us (8%)
  blocking collectives  16.1 us (2%)
  between operations  16 us (2%)
  starting transfers between devices  10.9 us (2%)
    psum x2, waiting for transfers between devices, residual_sum(): return lax.psum(gram(residual, residual), 'mesh')  198 us
    psum x1, waiting for transfers between devices, body(): lax.psum(jnp.einsum('bt,tsc->bsc', select, contrib, precision=highest).re...  121 us
    psum x1, waiting for transfers between devices, body(): curve = lax.psum(gram(direction, image), 'mesh')  105 us
    another operation x15, other arithmetic, solve(): return jax.scipy.linalg.cho_solve((jnp.linalg.cholesky(gmat), True), hmat)  68.6 us
    all_to_all x1, blocking collectives, body(): lead = lax.all_to_all(mine, 'elec', split_axis=0, concat_axis=1, tiled=True)  16.1 us
    dot_general x2, matrix products, body(): jnp.einsum('tij,tjc->tic', coupling, padded[targets], precision=highest)  15.2 us
    dot_general x2, matrix products, body(): jnp.einsum('tji,tjc->tic', coupling, blocks[tile_rows], precision=highest)  15.2 us
  transfers between devices with their start and end apart: 8, of which 6 were waited for; matrix products, arithmetic and copies ran while one was open for 9% of the time, Pallas kernels for 0%

commit v1 on v0

v1 whole, which is shorter than its diff:
```python
import functools

import jax
import jax.numpy as jnp
from jax import lax
from jax.experimental import pallas as pl
from jax.experimental.pallas import tpu as pltpu
from jax.sharding import PartitionSpec as P

HB = 2
SRCB_DEV = 2
BLK = 128
SHIFT = 2.0
F32 = jnp.float32
BF16 = jnp.bfloat16
HIGHEST = lax.Precision.HIGHEST


def mm(left, right, dims=((1,), (0,))):
    return lax.dot_general(left, right, (dims, ((), ())), preferred_element_type=F32)


def mmh(left, right, dims=((1,), (0,))):
    return lax.dot_general(
        left, right, (dims, ((), ())), preferred_element_type=F32, precision=HIGHEST
    )


def split(value):
    high = value.astype(BF16)
    return high, (value - high.astype(F32)).astype(BF16)


def rows_of(block):
    return block * BLK + lax.broadcasted_iota(jnp.int32, (BLK, BLK), 0)


def column(line):
    return jnp.transpose(jnp.broadcast_to(line, (BLK, BLK)))


def tile_loop(count, unroll, one):
    def group(g, carry):
        for k in range(unroll):
            one(g * unroll + k)
        return carry

    lax.fori_loop(0, count // unroll, group, 0)

    def rest(t, carry):
        one(t)
        return carry

    lax.fori_loop(count // unroll * unroll, count, rest, 0)


def first_kernel(
    trow, toff, tcount, ncount, rhs, diag, tiles, field, part, ahead, behind, acc, pieces
):
    rowb = rhs.shape[0] // BLK
    live = ncount[0]

    def prepare(b, carry):
        at = pl.ds(pl.multiple_of(b * BLK, BLK), BLK)
        value = jnp.where(rows_of(b) < live, rhs[at, :], 0.0)
        field[at, :] = value
        high, low = split(value)
        pieces[b, :BLK, :] = high
        pieces[b, BLK:, :] = low
        acc[b] = (column(diag[pl.ds(b, 1), :]) - SHIFT) * value
        return carry

    lax.fori_loop(0, rowb, prepare, 0)
    for b in range(rowb, rowb + HB):
        acc[b] = jnp.zeros((BLK, BLK), F32)
        pieces[b] = jnp.zeros((2 * BLK, BLK), BF16)

    def one(t):
        r = trow[t]
        c = r + toff[t]
        tile = tiles[t]
        flipped = jnp.transpose(tile)
        forward = mm(jnp.concatenate([tile, tile], 1), pieces[c])
        backward = mm(jnp.concatenate([flipped, flipped], 1), pieces[r])
        acc[r] += forward
        acc[c] += backward

    tile_loop(tcount[0], 4, one)

    def finish(b, carry):
        at = pl.ds(pl.multiple_of(b * BLK, BLK), BLK)
        part[at, :] = jnp.where(rows_of(b) < live, acc[b], 0.0)
        return carry

    lax.fori_loop(0, rowb, finish, 0)
    head = HB * BLK
    ahead[:head, :] = field[:head, :]
    ahead[head : 2 * head, :] = part[:head, :]
    ahead[2 * head :, :] = jnp.full((8, BLK), live.astype(F32))
    for b in range(HB):
        behind[b * BLK : (b + 1) * BLK, :] = acc[rowb + b]


def pack(first, second):
    i = lax.broadcasted_iota(jnp.int32, (BLK, BLK), 0)
    j = lax.broadcasted_iota(jnp.int32, (BLK, BLK), 1)
    line = jnp.sum(jnp.where(i == j, second, 0.0), 0, keepdims=True)
    return jnp.where(i <= j, first, second), line


def unpack(packed, line):
    i = lax.broadcasted_iota(jnp.int32, (BLK, BLK), 0)
    j = lax.broadcasted_iota(jnp.int32, (BLK, BLK), 1)
    flipped = jnp.transpose(packed)
    first = jnp.where(i <= j, packed, flipped)
    second = jnp.where(i > j, packed, flipped)
    return first, jnp.where(i == j, jnp.broadcast_to(line, (BLK, BLK)), second)


def second_kernel(
    trow, toff, tcount, ncount, core,
    field, part, diag, tiles, behind, from_behind, from_ahead,
    image, keep, give, acc, pieces, wide_h, wide_l, u_h, u_l,
):
    rowb = field.shape[0] // BLK
    live = ncount[0]
    count = tcount[0]
    head = HB * BLK
    edge = rowb - HB

    for b in range(HB):
        high, low = split(from_ahead[b * BLK : (b + 1) * BLK, :])
        pieces[rowb + b, :BLK, :] = high
        pieces[rowb + b, BLK:, :] = low
        acc[edge + b] = jnp.zeros((BLK, BLK), F32)

    def reach(t, carry):
        r = trow[t]
        c = r + toff[t]

        @pl.when(c >= rowb)
        def _():
            tile = tiles[t]
            acc[r] += mm(jnp.concatenate([tile, tile], 1), pieces[c])

        return carry

    lax.fori_loop(0, count, reach, 0)

    count_ahead = from_ahead[2 * head : 2 * head + 1, :]
    for b in range(HB):
        at = slice(b * BLK, (b + 1) * BLK)
        row = rows_of(b).astype(F32)
        value = from_ahead[head + b * BLK : head + (b + 1) * BLK, :]
        value = value + jnp.where(row < count_ahead, behind[at, :], 0.0)
        high, low = split(value)
        pieces[rowb + b, :BLK, :] = high
        pieces[rowb + b, BLK:, :] = low

    def settle(b, extra):
        at = pl.ds(pl.multiple_of(b * BLK, BLK), BLK)
        value = part[at, :]
        if extra is not None:
            value = value + jnp.where(rows_of(b) < live, extra, 0.0)
        image[at, :] = value
        high, low = split(value)
        pieces[b, :BLK, :] = high
        pieces[b, BLK:, :] = low
        wide_h[at, BLK:] = high
        wide_l[at, BLK:] = low
        high, low = split(field[at, :])
        wide_h[at, :BLK] = high
        wide_l[at, :BLK] = low
        acc[b] = (0.5 * (column(diag[pl.ds(b, 1), :]) - SHIFT)) * value

    for b in range(HB):
        settle(b, from_behind[b * BLK : (b + 1) * BLK, :])
    for b in range(edge, rowb):
        settle(b, acc[b])

    def middle(b, carry):
        settle(b, None)
        return carry

    lax.fori_loop(HB, edge, middle, 0)

    def one(t):
        r = trow[t]
        tile = tiles[t]
        acc[r] += mm(jnp.concatenate([tile, tile], 1), pieces[r + toff[t]])

    tile_loop(count, 4, one)

    def widen(b, carry):
        at = pl.ds(pl.multiple_of(b * BLK, BLK), BLK)
        high, low = split(acc[b])
        u_h[at, :] = high
        u_l[at, :] = low
        return carry

    lax.fori_loop(0, rowb, widen, 0)

    first = ((0,), (0,))
    straight = mm(wide_h[...], wide_h[...], first)
    cross = mm(wide_h[...], wide_l[...], first)
    n0 = straight[:BLK, :BLK] + cross[:BLK, :BLK] + jnp.transpose(cross[:BLK, :BLK])
    n1 = straight[:BLK, BLK:] + cross[:BLK, BLK:] + jnp.transpose(cross[BLK:, :BLK])
    n2 = straight[BLK:, BLK:] + cross[BLK:, BLK:] + jnp.transpose(cross[BLK:, BLK:])
    half = mm(wide_h[:, BLK:], u_h[...], first)
    half = half + mm(wide_h[:, BLK:], u_l[...], first) + mm(wide_l[:, BLK:], u_h[...], first)
    n3 = half + jnp.transpose(half)
    n1 = 0.5 * (n1 + jnp.transpose(n1))
    low_packed, low_line = pack(n0, n1)
    high_packed, high_line = pack(n2, n3)

    def place(low_ref, high_ref):
        low_ref[:BLK, :] = low_packed
        low_ref[BLK:, :] = jnp.broadcast_to(low_line, (8, BLK))
        high_ref[:BLK, :] = high_packed
        high_ref[BLK:, :] = jnp.broadcast_to(high_line, (8, BLK))

    @pl.when(core[0] == 0)
    def _():
        place(keep, give)

    @pl.when(core[0] != 0)
    def _():
        place(give, keep)


def invert(matrix):
    n = matrix.shape[0]
    step = 8
    lane = lax.broadcasted_iota(jnp.int32, (step, n), 1)
    sub = lax.broadcasted_iota(jnp.int32, (step, n), 0)
    for k in range(n // step):
        base = k * step
        panel = matrix[base : base + step, :]
        inside = (lane >= base) & (lane < base + step)
        unit = (lane - base == sub).astype(F32)
        work, extra = panel, unit
        for j in range(step):
            factor = work[:, base + j : base + j + 1]
            scale = 1.0 / factor[j : j + 1, :]
            row = work[j : j + 1, :] * scale
            other = extra[j : j + 1, :] * scale
            here = sub == j
            work = jnp.where(here, row, work - factor * row)
            extra = jnp.where(here, other, extra - factor * other)
        outer = jnp.where(inside, 0.0, panel)
        rows = jnp.where(inside, -extra, work)
        matrix = jnp.where(inside[:1, :], 0.0, matrix) - mmh(outer, rows, ((0,), (0,)))
        pieces = []
        if base:
            pieces.append(matrix[:base, :])
        pieces.append(rows)
        if base + step < n:
            pieces.append(matrix[base + step :, :])
        matrix = jnp.concatenate(pieces, 0)
    return -matrix


def solve_kernel(core, mine, other, out):
    first = core[0] == 0
    low = jnp.where(first, mine[...], other[...])
    high = jnp.where(first, other[...], mine[...])
    n0, n1 = unpack(low[:BLK, :], low[BLK : BLK + 1, :])
    n2, n3 = unpack(high[:BLK, :], high[BLK : BLK + 1, :])
    m1 = n1 + SHIFT * n0
    m2 = n2 + SHIFT * n1
    m3 = n3 + SHIFT * n2
    inverse = invert(m1)
    both = mmh(inverse, jnp.concatenate([m2, n0], 1))
    across = mmh(m2, both)
    schur = m3 - across[:, :BLK]
    y1 = mmh(invert(schur), n1 - across[:, BLK:])
    y0 = both[:, BLK:] - mmh(both[:, :BLK], y1)
    out[:BLK, :] = y0
    out[BLK:, :] = y1


def third_kernel(irow, iblk, core, field, image, coef, inc, sol, keep, give, pieces):
    rowb = field.shape[0] // BLK
    y0h, y0l = split(coef[:BLK, :])
    y1h, y1l = split(coef[BLK:, :])
    stack_h = jnp.concatenate([y0h, y1h], 0)
    stack_l = jnp.concatenate([y0l, y1l], 0)
    keep[...] = jnp.zeros(keep.shape, F32)
    give[...] = jnp.zeros(give.shape, F32)

    def combine(b, carry):
        at = pl.ds(pl.multiple_of(b * BLK, BLK), BLK)
        fh, fl = split(field[at, :])
        ih, il = split(image[at, :])
        left_h = jnp.concatenate([fh, ih], 1)
        left_l = jnp.concatenate([fl, il], 1)
        value = mm(left_h, stack_h) + (mm(left_h, stack_l) + mm(left_l, stack_h))
        sol[at, :] = value
        high, low = split(value)
        pieces[b, :BLK, :] = high
        pieces[b, BLK:, :] = low
        return carry

    lax.fori_loop(0, rowb, combine, 0)

    def add(u, carry):
        flipped = jnp.transpose(inc[u])
        product = mm(jnp.concatenate([flipped, flipped], 1), pieces[irow[u]])
        block = iblk[u]
        owner = block // SRCB_DEV
        at = owner // 2 * SRCB_DEV + block % SRCB_DEV
        mine = owner % 2 == core[0]

        @pl.when(mine)
        def _():
            keep[at] += product

        @pl.when(jnp.logical_not(mine))
        def _():
            give[at] += product

        return carry

    lax.fori_loop(0, inc.shape[0], add, 0)


def call(kernel, n_scalar, n_vector, outs, scratch=()):
    vmem = pl.BlockSpec(memory_space=pltpu.VMEM)
    smem = pl.BlockSpec(memory_space=pltpu.SMEM)
    return pl.pallas_call(
        kernel,
        in_specs=[smem] * n_scalar + [vmem] * n_vector,
        out_specs=[vmem] * len(outs),
        out_shape=[jax.ShapeDtypeStruct(shape, F32) for shape in outs],
        scratch_shapes=[pltpu.VMEM(shape, dtype) for shape, dtype in scratch],
        compiler_params=pltpu.CompilerParams(vmem_limit_bytes=48 * 1024 * 1024),
    )


def body(
    sides, rhs, diagonal, tile_values, tile_rows, tile_offsets, tile_count, node_count,
    inc_values, inc_rows, inc_blocks,
):
    nx, ny = sides
    nodes, width = rhs.shape
    rowb = nodes // BLK
    head = HB * BLK
    count = 2 * nx * ny
    lead_half = nx * ny * SRCB_DEV
    core = (lax.axis_index("mesh") % 2).astype(jnp.int32)[None]
    diag = diagonal.reshape(rowb, BLK)

    def place(x, y, c):
        return (x % nx * ny + y % ny) * 2 + c

    def moved(value, dx, dy):
        return lax.ppermute(value, "mesh", [
            (place(x, y, c), place(x + dx, y + dy, c))
            for x in range(nx) for y in range(ny) for c in range(2)
        ])

    def swap(value):
        return lax.ppermute(value, "mesh", [(i, i ^ 1) for i in range(count)])

    field, part, ahead, behind = call(
        first_kernel, 4, 3,
        [(nodes, width), (nodes, width), (2 * head + 8, width), (head, width)],
        [((rowb + HB, BLK, BLK), F32), ((rowb + HB, 2 * BLK, BLK), BF16)],
    )(tile_rows, tile_offsets, tile_count, node_count, rhs, diag, tile_values)
    from_ahead = lax.ppermute(ahead, "mesh", [(i + 1, i) for i in range(count - 1)])
    from_behind = lax.ppermute(behind, "mesh", [(i, i + 1) for i in range(count - 1)])
    image, keep, give = call(
        second_kernel, 5, 7,
        [(nodes, width), (BLK + 8, BLK), (BLK + 8, BLK)],
        [
            ((rowb + HB, BLK, BLK), F32), ((rowb + HB, 2 * BLK, BLK), BF16),
            ((nodes, 2 * BLK), BF16), ((nodes, 2 * BLK), BF16),
            ((nodes, BLK), BF16), ((nodes, BLK), BF16),
        ],
    )(tile_rows, tile_offsets, tile_count, node_count, core,
      field, part, diag, tile_values, behind, from_behind, from_ahead)
    total = keep + swap(give)
    total = total + functools.reduce(jnp.add, [moved(total, d, 0) for d in range(1, nx)])
    total = total + functools.reduce(jnp.add, [moved(total, 0, d) for d in range(1, ny)])
    (coef,) = call(solve_kernel, 1, 2, [(2 * BLK, BLK)])(core, total, swap(total))
    solution, keep, give = call(
        third_kernel, 3, 4,
        [(nodes, width), (lead_half, BLK, BLK), (lead_half, BLK, BLK)],
        [((rowb, 2 * BLK, BLK), BF16)],
    )(inc_rows, inc_blocks, core, field, image, coef, inc_values)
    half = (keep + swap(give)).reshape(nx * ny, SRCB_DEV * BLK, width)
    groups = [[2 * i + c for i in range(nx * ny)] for c in range(2)]
    got = lax.all_to_all(
        half, "mesh", split_axis=0, concat_axis=0, tiled=True, axis_index_groups=groups
    )
    lead = lax.all_to_all(got.sum(0), "elec", split_axis=0, concat_axis=1, tiled=True)
    return solution, lead


def solution(mesh):
    placed = (
        P("mesh", "elec"),
        P("mesh"),
        P("mesh", None, None),
        P("mesh"),
        P("mesh"),
        P("mesh"),
        P("mesh"),
        P("mesh", None, None),
        P("mesh"),
        P("mesh"),
    )
    return jax.shard_map(
        functools.partial(body, (4, 4)),
        mesh=mesh,
        in_specs=placed,
        out_specs=(P("mesh", "elec"), P(("mesh", "elec"), None)),
        check_vma=False,
    )
```

time: 683 us -> 151 us (0.22)
  waiting for transfers between devices: 430 us -> 19.7 us
  other arithmetic: 77.7 us -> 0.5 us
  matrix products: 71.1 us -> 0 us
  Pallas kernels: 0 us -> 54.6 us
  local copies, waits for them, and re-layouts: 54 us -> 8.34 us
  blocking collectives: 16.1 us -> 49.5 us
  between operations: 16 us -> 2.1 us
    psum x4 -> x0, waiting for transfers between devices: 424 us -> none  [the longest x2 198 us: residual_sum(): return lax.psum(gram(residual, residual), 'mesh')]
    another operation x15 -> x0, other arithmetic: 68.6 us -> none  [solve(): return jax.scipy.linalg.cho_solve((jnp.linalg.cholesky(gmat), True), hmat)]
    dot_general x18 -> x0, matrix products: 68 us -> none  [the longest x2 15.2 us: body(): jnp.einsum('tij,tjc->tic', coupling, padded[targets], precision=highest)]
    pallas_call x0 -> x4, Pallas kernels: none -> 54.6 us  [the longest x1 28.8 us: body(): coef, = call(solve_kernel, 1, 2, [(2 * BLK, BLK)])(core, total, swap(total))]
    all_to_all x1 -> x2, blocking collectives: 16.1 us -> 49.5 us  [the longest x1 32.2 us: body(): lax.all_to_all(half, 'mesh', split_axis=0, concat_axis=0, tiled=True, axi...]
    dot_general x6 -> x0, local copies, waits for them, and re-layouts: 29 us -> none  [the longest x2 11.1 us: body(): jnp.einsum('tji,tjc->tic', coupling, blocks[tile_rows], precision=highest)]
    gather x5 -> x0, local copies, waits for them, and re-layouts: 16.7 us -> none  [the longest x2 8.22 us: body(): padded[targets]]
    ppermute x4 -> x11, waiting for transfers between devices: 5.85 us -> 19.7 us  [the longest x6 8.78 us: moved(): lax.ppermute(value, 'mesh', [(place(x, y, c), place(x + dx, y + dy, c)) f...]
  transfers between devices with their start and end apart: 8 -> 11, of which waited for: 6 -> 8; matrix products, arithmetic and copies ran while one was open for 9% -> 0% of each run, Pallas kernels for 0% -> 0%
where the time goes in v1:
time: 151 us; the launch traced here: 150 us
  Pallas kernels  54.6 us (36%)
  blocking collectives  49.5 us (33%)
  waiting for transfers between devices  19.7 us (13%)
  starting transfers between devices  15.4 us (10%)
  local copies, waits for them, and re-layouts  8.34 us (6%)
  between operations  2.1 us (1%)
    all_to_all x1, blocking collectives, body(): lax.all_to_all(half, 'mesh', split_axis=0, concat_axis=0, tiled=True, axi...  32.2 us
    pallas_call x1, Pallas kernels, body(): coef, = call(solve_kernel, 1, 2, [(2 * BLK, BLK)])(core, total, swap(total))  28.8 us
    all_to_all x1, blocking collectives, body(): lax.all_to_all(got.sum(0), 'elec', split_axis=0, concat_axis=1, tiled=True)  17.4 us
    ppermute x6, starting transfers between devices, moved(): lax.ppermute(value, 'mesh', [(place(x, y, c), place(x + dx, y + dy, c)) f...  10.5 us
    pallas_call x1, Pallas kernels, body(): call(third_kernel, 3, 4, [(nodes, width), (lead_half, BLK, BLK), (lead_ha...  9 us
    ppermute x6, waiting for transfers between devices, moved(): lax.ppermute(value, 'mesh', [(place(x, y, c), place(x + dx, y + dy, c)) f...  8.78 us
    pallas_call x1, Pallas kernels, body(): call(second_kernel, 5, 7, [(nodes, width), (BLK + 8, BLK), (BLK + 8, BLK)...  8.76 us
    pallas_call x1, Pallas kernels, body(): call(first_kernel, 4, 3, [(nodes, width), (nodes, width), (2 * head + 8,...  8.03 us
  transfers between devices with their start and end apart: 11, of which 8 were waited for; matrix products, arithmetic and copies ran while one was open for 0% of the time, Pallas kernels for 0%

profile of v1, /device:TPU:8, one launch (start us, length us, event | category | flops | bytes accessed | tf_op | source)
XLA Modules:
  0.0 150.1 jit_solution(9410300287634560525)
XLA Ops:
  0.6 0.0 copy-start.9
  1.9 0.0 copy-start
  2.0 1.6 %copy-done = bf16[64,128,128]{2,1,0:T(8,128)(2,1)S(1)} copy-done((bf16[64,128,128]{2,1,0:T(8,128)(2,1)S(1)}, bf16[64,128,128]{2,1,0:T(8,128)(2,1)}, u32[]{:S(2)}) %copy-start) | copy-done | bytes 2097176
  3.5 0.0 copy-start.2
  3.5 1.2 copy-done.2
  4.8 0.0 copy-start.6
  4.8 0.7 copy-done.6
  5.5 0.0 copy-start.8
  5.5 0.7 copy-done.8
  6.1 0.0 copy-start.10
  6.1 0.7 copy-done.10
  6.8 0.0 copy-start.1
  6.8 0.0 copy-start.7
  6.8 8.0 %shard_map.113 = (f32[2048,128]{1,0:T(8,128)S(1)}, f32[2048,128]{1,0:T(8,128)S(1)}, f32[520,128]{1,0:T(8,128)}, f32[256,128]{1,0:T(8,128)S(1)}) custom-call(s32[64]{0:T(128)S(1)} %copy-done.8, s32[64]{0:T(128)S(1)} %copy-done.10, s32[1]{0:T(128)S(6)} %copy.15.tcount, s32[1]{0:T(128)S(6)} %copy.16.ncount, f32[2048,128]{1,0:T(8,128)S(1)} %copy-done.2, ...), custom_call_target="tpu_custom_call" | custom-call | tf_op jit(solution)/shard_map/pallas_call | solution.py:365
  14.8 0.0 copy-start.3
  14.8 1.0 copy-done.3
  15.8 1.9 %collective-permute-start.1 = (f32[520,128]{1,0:T(8,128)}, f32[520,128]{1,0:T(8,128)S(1)}, u32[]{:S(2)}, u32[]{:S(2)}) collective-permute-start(f32[520,128]{1,0:T(8,128)} %get-tuple-element.15), channel_id=1, source_target_pairs={{8,0},{16,8},{24,16},{32,24},{40,32},{48,40},{56,48},{64,56},{72,6... | collective-permute-start | bytes 798728 | tf_op jit(solution)/shard_map/ppermute | solution.py:370
  17.7 2.4 %collective-permute-start = (f32[256,128]{1,0:T(8,128)S(1)}, f32[256,128]{1,0:T(8,128)}, u32[]{:S(2)}, u32[]{:S(2)}) collective-permute-start(f32[256,128]{1,0:T(8,128)S(1)} %get-tuple-element.14.behind), channel_id=1, source_target_pairs={{0,8},{8,16},{16,24},{24,32},{32,40},{40,48},{48,56},{56,64},{64,7... | collective-permute-start | bytes 393224 | tf_op jit(solution)/shard_map/ppermute | solution.py:371
  20.1 4.2 %collective-permute-done.from_behind = f32[256,128]{1,0:T(8,128)} collective-permute-done((f32[256,128]{1,0:T(8,128)S(1)}, f32[256,128]{1,0:T(8,128)}, u32[]{:S(2)}, u32[]{:S(2)}) %collective-permute-start) | collective-permute-done | bytes 131104 | tf_op jit(solution)/shard_map/ppermute | solution.py:371
  24.3 0.0 collective-permute-done.1.from_ahead
  24.3 0.0 copy-done.9
  24.3 0.0 copy-done.1
  24.3 0.0 copy-done.7
  24.3 0.0 copy-start.4
  24.3 1.2 copy-done.4
  25.6 0.0 copy-start.11
  25.6 0.7 copy-done.11
  26.2 0.0 copy-start.5
  26.2 0.0 copy-start.12
  26.2 0.0 copy-start.13
  26.2 8.8 %shard_map.114 = (f32[2048,128]{1,0:T(8,128)S(1)}, f32[136,128]{1,0:T(8,128)S(1)}, f32[136,128]{1,0:T(8,128)S(1)}) custom-call(s32[64]{0:T(128)S(1)} %copy-done.9, s32[64]{0:T(128)S(1)} %copy-done.11, s32[1]{0:T(128)S(6)} %copy.15.tcount, s32[1]{0:T(128)S(6)} %copy.16.ncount, s32[1]{0:T(128)} %bitcast.core, f32[2048,128]{1,0:T(8,128)S(1)} %get-tuple-element.12.field, ...), custom_call_target="tpu_custom_call" | custom-call | tf_op jit(solution)/shard_map/pallas_call | solution.py:372
  35.0 0.1 collective-permute-start.2
  35.1 1.2 collective-permute-done.2
  36.3 0.1 collective-permute-start.5
  36.4 0.2 collective-permute-start.4
  36.6 1.8 %collective-permute-start.3 = (f32[136,128]{1,0:T(8,128)S(1)}, f32[136,128]{1,0:T(8,128)S(1)}, u32[]{:S(2)}, u32[]{:S(2)}) collective-permute-start(f32[136,128]{1,0:T(8,128)S(1)} %add.29), channel_id=1, source_target_pairs={{0,64},{8,72},{16,80},{24,88},{32,96},{40,104},{48,112},{56,120},{... | collective-permute-start | bytes 208904 | tf_op jit(solution)/shard_map/ppermute | solution.py:357
  38.5 3.0 %collective-permute-done.5 = f32[136,128]{1,0:T(8,128)S(1)} collective-permute-done((f32[136,128]{1,0:T(8,128)S(1)}, f32[136,128]{1,0:T(8,128)S(1)}, u32[]{:S(2)}, u32[]{:S(2)}) %collective-permute-start.5) | collective-permute-done | bytes 69664 | tf_op jit(solution)/shard_map/ppermute | solution.py:357
  41.4 1.0 collective-permute-done.4
  42.4 1.4 collective-permute-done.3
  43.8 6.0 %collective-permute-start.8 = (f32[136,128]{1,0:T(8,128)S(1)}, f32[136,128]{1,0:T(8,128)S(1)}, u32[]{:S(2)}, u32[]{:S(2)}) collective-permute-start(f32[136,128]{1,0:T(8,128)S(1)} %add_add_fusion.1), channel_id=1, source_target_pairs={{0,48},{8,56},{16,0},{24,8},{32,16},{40,24},{48,32},{56,40},{64,11... | collective-permute-start | bytes 208904 | tf_op jit(solution)/shard_map/ppermute | solution.py:357
  49.9 0.0 collective-permute-start.7
  49.9 2.4 %collective-permute-start.6 = (f32[136,128]{1,0:T(8,128)S(1)}, f32[136,128]{1,0:T(8,128)S(1)}, u32[]{:S(2)}, u32[]{:S(2)}) collective-permute-start(f32[136,128]{1,0:T(8,128)S(1)} %add_add_fusion.1), channel_id=1, source_target_pairs={{0,16},{8,24},{16,32},{24,40},{32,48},{40,56},{48,0},{56,8},{64,80... | collective-permute-start | bytes 208904 | tf_op jit(solution)/shard_map/ppermute | solution.py:357
  52.3 0.0 collective-permute-done.8
  52.3 3.4 %collective-permute-done.7 = f32[136,128]{1,0:T(8,128)S(1)} collective-permute-done((f32[136,128]{1,0:T(8,128)S(1)}, f32[136,128]{1,0:T(8,128)S(1)}, u32[]{:S(2)}, u32[]{:S(2)}) %collective-permute-start.7) | collective-permute-done | bytes 69664 | tf_op jit(solution)/shard_map/ppermute | solution.py:357
  55.7 0.0 collective-permute-done.6
  55.7 0.3 collective-permute-start.9
  56.0 1.2 collective-permute-done.9.other
  57.2 28.8 %shard_map.115.coef = f32[256,128]{1,0:T(8,128)S(1)} custom-call(s32[1]{0:T(128)} %bitcast.core, f32[136,128]{1,0:T(8,128)S(1)} %add_add_fusion.mine, f32[136,128]{1,0:T(8,128)S(1)} %collective-permute-done.9.other), custom_call_target="tpu_custom_call" | custom-call | tf_op jit(solution)/shard_map/pallas_call | solution.py:385
  86.0 0.0 copy-done.5
  86.0 0.0 copy-done.12
  86.0 0.0 copy-done.13
  86.1 9.0 %shard_map.116 = (f32[2048,128]{1,0:T(8,128)}, f32[32,128,128]{2,1,0:T(8,128)S(1)}, f32[32,128,128]{2,1,0:T(8,128)}) custom-call(s32[16]{0:T(128)S(1)} %copy-done.12, s32[16]{0:T(128)S(1)} %copy-done.13, s32[1]{0:T(128)} %bitcast.core, f32[2048,128]{1,0:T(8,128)S(1)} %get-tuple-element.12.field, f32[2048,128]{1,0:T(8,128)S(1)} %get-tuple-element.16.image, ...), custom_call_target="tpu_custom_call" | custom-call | tf_op jit(solution)/shard_map/pallas_call | solution.py:386
  95.0 0.2 collective-permute-start.10
  95.2 4.2 %collective-permute-done.10 = f32[32,128,128]{2,1,0:T(8,128)S(1)} collective-permute-done((f32[32,128,128]{2,1,0:T(8,128)}, f32[32,128,128]{2,1,0:T(8,128)S(1)}, u32[]{:S(2)}, u32[]{:S(2)}) %collective-permute-start.10) | collective-permute-done | bytes 2097184 | tf_op jit(solution)/shard_map/ppermute | solution.py:363
  99.4 0.3 add.36
  99.8 32.2 %all_to_all.24 = f32[16,256,128]{2,1,0:T(8,128)S(1)} all-to-all(f32[16,256,128]{2,1,0:T(8,128)S(1)} %bitcast.12), channel_id=1, replica_groups={{0,16,32,48,64,80,96,112,128,144,160,176,192,208,224,240},{8,24,40,56,7..., dimensions={0} | all-to-all | bytes 4194304 | tf_op jit(solution)/shard_map/all_to_all | solution.py:393
  131.9 0.1 reduce_sum.9
  132.1 17.4 %all_to_all.25 = f32[8,32,128]{2,1,0:T(8,128)S(1)} all-to-all(f32[8,32,128]{2,1,0:T(8,128)S(1)} %bitcast.13), channel_id=1, replica_groups=mesh['mesh'=32,'elec'=8] {'elec'}, dimensions={0} | all-to-all | bytes 262144 | tf_op jit(solution)/shard_map/all_to_all | solution.py:396
  149.4 0.7 copy_bitcast_fusion
  (3 shorter events, 0.1 us)
Async XLA Ops:
  0.6 23.7 %copy-start.9 = (s32[64]{0:T(128)S(1)}, s32[64]{0:T(128)}, u32[]{:S(2)}) copy-start(s32[64]{0:T(128)} %trow.3) | copy-start | bytes 772
  1.9 1.6 %copy-start = (bf16[64,128,128]{2,1,0:T(8,128)(2,1)S(1)}, bf16[64,128,128]{2,1,0:T(8,128)(2,1)}, u32[]{:S(2)}) copy-start(bf16[64,128,128]{2,1,0:T(8,128)(2,1)} %tiles.3) | copy-start | bytes 6291460
  3.5 1.2 copy-start.2
  4.8 0.7 copy-start.6
  5.5 0.7 copy-start.8
  6.1 0.7 copy-start.10
  6.8 17.5 %copy-start.1 = (bf16[64,128,128]{2,1,0:T(8,128)(2,1)S(1)}, bf16[64,128,128]{2,1,0:T(8,128)(2,1)}, u32[]{:S(2)}) copy-start(bf16[64,128,128]{2,1,0:T(8,128)(2,1)} %tiles.3) | copy-start | bytes 6291460
  6.8 17.5 %copy-start.7 = (f32[2048]{0:T(1024)S(1)}, f32[2048]{0:T(1024)}, u32[]{:S(2)}) copy-start(f32[2048]{0:T(1024)} %param.11) | copy-start | bytes 24580
  14.8 1.0 copy-start.3
  15.8 8.5 %collective-permute-start.1 = (f32[520,128]{1,0:T(8,128)}, f32[520,128]{1,0:T(8,128)S(1)}, u32[]{:S(2)}, u32[]{:S(2)}) collective-permute-start(f32[520,128]{1,0:T(8,128)} %get-tuple-element.15), channel_id=1, source_target_pairs={{8,0},{16,8},{24,16},{32,24},{40,32},{48,40},{56,48},{64,56},{72,6... | collective-permute-start | bytes 798728 | tf_op jit(solution)/shard_map/ppermute | solution.py:370
  17.7 6.6 %collective-permute-start = (f32[256,128]{1,0:T(8,128)S(1)}, f32[256,128]{1,0:T(8,128)}, u32[]{:S(2)}, u32[]{:S(2)}) collective-permute-start(f32[256,128]{1,0:T(8,128)S(1)} %get-tuple-element.14.behind), channel_id=1, source_target_pairs={{0,8},{8,16},{16,24},{24,32},{32,40},{40,48},{48,56},{56,64},{64,7... | collective-permute-start | bytes 393224 | tf_op jit(solution)/shard_map/ppermute | solution.py:371
  24.3 1.2 copy-start.4
  25.6 0.7 copy-start.11
  26.2 59.8 %copy-start.5 = (bf16[16,128,128]{2,1,0:T(8,128)(2,1)S(1)}, bf16[16,128,128]{2,1,0:T(8,128)(2,1)}, u32[]{:S(2)}) copy-start(bf16[16,128,128]{2,1,0:T(8,128)(2,1)} %inc.1) | copy-start | bytes 1572868
  26.2 59.8 %copy-start.12 = (s32[16]{0:T(128)S(1)}, s32[16]{0:T(128)}, u32[]{:S(2)}) copy-start(s32[16]{0:T(128)} %irow.1) | copy-start | bytes 196
  26.2 59.8 %copy-start.13 = (s32[16]{0:T(128)S(1)}, s32[16]{0:T(128)}, u32[]{:S(2)}) copy-start(s32[16]{0:T(128)} %iblk.1) | copy-start | bytes 196
  35.0 1.3 collective-permute-start.2
  36.3 5.1 %collective-permute-start.5 = (f32[136,128]{1,0:T(8,128)S(1)}, f32[136,128]{1,0:T(8,128)S(1)}, u32[]{:S(2)}, u32[]{:S(2)}) collective-permute-start(f32[136,128]{1,0:T(8,128)S(1)} %add.29), channel_id=1, source_target_pairs={{0,192},{8,200},{16,208},{24,216},{32,224},{40,232},{48,240},{56,2... | collective-permute-start | bytes 208904 | tf_op jit(solution)/shard_map/ppermute | solution.py:357
  36.4 6.0 %collective-permute-start.4 = (f32[136,128]{1,0:T(8,128)S(1)}, f32[136,128]{1,0:T(8,128)S(1)}, u32[]{:S(2)}, u32[]{:S(2)}) collective-permute-start(f32[136,128]{1,0:T(8,128)S(1)} %add.29), channel_id=1, source_target_pairs={{0,128},{8,136},{16,144},{24,152},{32,160},{40,168},{48,176},{56,1... | collective-permute-start | bytes 208904 | tf_op jit(solution)/shard_map/ppermute | solution.py:357
  36.6 7.2 %collective-permute-start.3 = (f32[136,128]{1,0:T(8,128)S(1)}, f32[136,128]{1,0:T(8,128)S(1)}, u32[]{:S(2)}, u32[]{:S(2)}) collective-permute-start(f32[136,128]{1,0:T(8,128)S(1)} %add.29), channel_id=1, source_target_pairs={{0,64},{8,72},{16,80},{24,88},{32,96},{40,104},{48,112},{56,120},{... | collective-permute-start | bytes 208904 | tf_op jit(solution)/shard_map/ppermute | solution.py:357
  43.8 8.4 %collective-permute-start.8 = (f32[136,128]{1,0:T(8,128)S(1)}, f32[136,128]{1,0:T(8,128)S(1)}, u32[]{:S(2)}, u32[]{:S(2)}) collective-permute-start(f32[136,128]{1,0:T(8,128)S(1)} %add_add_fusion.1), channel_id=1, source_target_pairs={{0,48},{8,56},{16,0},{24,8},{32,16},{40,24},{48,32},{56,40},{64,11... | collective-permute-start | bytes 208904 | tf_op jit(solution)/shard_map/ppermute | solution.py:357
  49.9 5.8 %collective-permute-start.7 = (f32[136,128]{1,0:T(8,128)S(1)}, f32[136,128]{1,0:T(8,128)S(1)}, u32[]{:S(2)}, u32[]{:S(2)}) collective-permute-start(f32[136,128]{1,0:T(8,128)S(1)} %add_add_fusion.1), channel_id=1, source_target_pairs={{0,32},{8,40},{16,48},{24,56},{32,0},{40,8},{48,16},{56,24},{64,96... | collective-permute-start | bytes 208904 | tf_op jit(solution)/shard_map/ppermute | solution.py:357
  49.9 5.8 %collective-permute-start.6 = (f32[136,128]{1,0:T(8,128)S(1)}, f32[136,128]{1,0:T(8,128)S(1)}, u32[]{:S(2)}, u32[]{:S(2)}) collective-permute-start(f32[136,128]{1,0:T(8,128)S(1)} %add_add_fusion.1), channel_id=1, source_target_pairs={{0,16},{8,24},{16,32},{24,40},{32,48},{40,56},{48,0},{56,8},{64,80... | collective-permute-start | bytes 208904 | tf_op jit(solution)/shard_map/ppermute | solution.py:357
  55.7 1.5 %collective-permute-start.9 = (f32[136,128]{1,0:T(8,128)S(1)}, f32[136,128]{1,0:T(8,128)S(1)}, u32[]{:S(2)}, u32[]{:S(2)}) collective-permute-start(f32[136,128]{1,0:T(8,128)S(1)} %add_add_fusion.mine), channel_id=1, source_target_pairs={{0,8},{8,0},{16,24},{24,16},{32,40},{40,32},{48,56},{56,48},{64,72... | collective-permute-start | bytes 208904 | tf_op jit(solution)/shard_map/ppermute | solution.py:363
  95.0 4.4 %collective-permute-start.10 = (f32[32,128,128]{2,1,0:T(8,128)}, f32[32,128,128]{2,1,0:T(8,128)S(1)}, u32[]{:S(2)}, u32[]{:S(2)}) collective-permute-start(f32[32,128,128]{2,1,0:T(8,128)} %get-tuple-element.21), channel_id=1, source_target_pairs={{0,8},{8,0},{16,24},{24,16},{32,40},{40,32},{48,56},{56,48},{64,72... | collective-permute-start | bytes 6291464 | tf_op jit(solution)/shard_map/ppermute | solution.py:363

commit v2 on v1

--- a/solution.py
+++ b/solution.py
@@ -54,9 +54,26 @@
     lax.fori_loop(count // unroll * unroll, count, rest, 0)
 
 
+def fetch(pairs, sems):
+    copies = [
+        pltpu.make_async_copy(source, target, sems.at[i])
+        for i, (source, target) in enumerate(pairs)
+    ]
+    for copy in copies:
+        copy.start()
+    return copies
+
+
 def first_kernel(
-    trow, toff, tcount, ncount, rhs, diag, tiles, field, part, ahead, behind, acc, pieces
+    tcount, ncount, trow_far, toff_far, rhs_far, diag_far, tiles_far,
+    field, part, ahead, behind, acc, pieces, trow, toff, rhs, diag, tiles, sems,
 ):
+    get_rhs, get_diag, get_row, get_off, get_tiles = fetch(
+        [(rhs_far, rhs), (diag_far, diag), (trow_far, trow), (toff_far, toff), (tiles_far, tiles)],
+        sems,
+    )
+    get_rhs.wait()
+    get_diag.wait()
     rowb = rhs.shape[0] // BLK
     live = ncount[0]
 
@@ -74,6 +91,9 @@
     for b in range(rowb, rowb + HB):
         acc[b] = jnp.zeros((BLK, BLK), F32)
         pieces[b] = jnp.zeros((2 * BLK, BLK), BF16)
+    get_row.wait()
+    get_off.wait()
+    get_tiles.wait()
 
     def one(t):
         r = trow[t]
@@ -118,10 +138,13 @@
 
 
 def second_kernel(
-    trow, toff, tcount, ncount, core,
-    field, part, diag, tiles, behind, from_behind, from_ahead,
-    image, keep, give, acc, pieces, wide_h, wide_l, u_h, u_l,
+    tcount, ncount, core,
+    trow_far, toff_far, diag_far, tiles_far, field, part, behind, from_behind, from_ahead,
+    image, keep, give, acc, pieces, wide_h, wide_l, u_h, u_l, trow, toff, diag, tiles, sems,
 ):
+    get_row, get_off, get_diag, get_tiles = fetch(
+        [(trow_far, trow), (toff_far, toff), (diag_far, diag), (tiles_far, tiles)], sems
+    )
     rowb = field.shape[0] // BLK
     live = ncount[0]
     count = tcount[0]
@@ -133,6 +156,9 @@
         pieces[rowb + b, :BLK, :] = high
         pieces[rowb + b, BLK:, :] = low
         acc[edge + b] = jnp.zeros((BLK, BLK), F32)
+
+    for copy in (get_row, get_off, get_diag, get_tiles):
+        copy.wait()
 
     def reach(t, carry):
         r = trow[t]
@@ -228,34 +254,68 @@
         place(give, keep)
 
 
+def pivot_block(entry, n):
+    for p in range(n):
+        scale = pl.reciprocal(entry[p, p])
+        old = {i: entry[min(i, p), max(i, p)] for i in range(n) if i != p}
+        new = {i: value * scale for i, value in old.items()}
+        for i in range(n):
+            for j in range(i, n):
+                if i == p and j == p:
+                    entry[i, j] = -scale
+                elif i == p or j == p:
+                    entry[i, j] = new[i + j - p]
+                else:
+                    entry[i, j] = entry[i, j] - new[i] * old[j]
+    return entry
+
+
 def invert(matrix):
     n = matrix.shape[0]
     step = 8
     lane = lax.broadcasted_iota(jnp.int32, (step, n), 1)
     sub = lax.broadcasted_iota(jnp.int32, (step, n), 0)
+    masks = [sub == i for i in range(step)]
+    panel = matrix[:step, :]
     for k in range(n // step):
         base = k * step
-        panel = matrix[base : base + step, :]
         inside = (lane >= base) & (lane < base + step)
-        unit = (lane - base == sub).astype(F32)
-        work, extra = panel, unit
+        columns = [
+            jnp.broadcast_to(panel[:, base + j : base + j + 1], (step, n)) for j in range(step)
+        ]
+        entry = {
+            (i, j): jnp.broadcast_to(columns[j][i : i + 1, :], (step, n))
+            for i in range(step) for j in range(i, step)
+        }
+        entry = pivot_block(entry, step)
+        rows = None
+        unit = None
         for j in range(step):
-            factor = work[:, base + j : base + j + 1]
-            scale = 1.0 / factor[j : j + 1, :]
-            row = work[j : j + 1, :] * scale
-            other = extra[j : j + 1, :] * scale
-            here = sub == j
-            work = jnp.where(here, row, work - factor * row)
-            extra = jnp.where(here, other, extra - factor * other)
+            weight = entry[0, j]
+            for i in range(1, step):
+                weight = jnp.where(masks[i], entry[min(i, j), max(i, j)], weight)
+            term = weight * panel[j : j + 1, :]
+            rows = term if rows is None else rows + term
+            spot = jnp.where(lane == base + j, weight, 0.0)
+            unit = spot if unit is None else unit + spot
+        rows = jnp.where(inside, unit, -rows)
         outer = jnp.where(inside, 0.0, panel)
-        rows = jnp.where(inside, -extra, work)
-        matrix = jnp.where(inside[:1, :], 0.0, matrix) - mmh(outer, rows, ((0,), (0,)))
+        cleared = jnp.where(inside[:1, :], 0.0, matrix)
+        if k + 1 < n // step:
+            ahead = matrix[base + step : base + 2 * step, :]
+            panel = cleared[base + step : base + 2 * step, :]
+            for j in range(step):
+                factor = jnp.broadcast_to(ahead[:, base + j : base + j + 1], (step, n))
+                panel = panel - factor * rows[j : j + 1, :]
+        matrix = cleared - mmh(outer, rows, ((0,), (0,)))
         pieces = []
         if base:
             pieces.append(matrix[:base, :])
         pieces.append(rows)
         if base + step < n:
-            pieces.append(matrix[base + step :, :])
+            pieces.append(panel)
+        if base + 2 * step < n:
+            pieces.append(matrix[base + 2 * step :, :])
         matrix = jnp.concatenate(pieces, 0)
     return -matrix
 
@@ -324,16 +384,17 @@
     lax.fori_loop(0, inc.shape[0], add, 0)
 
 
-def call(kernel, n_scalar, n_vector, outs, scratch=()):
+def call(kernel, n_scalar, n_far, n_vector, outs, scratch=(), mib=16):
     vmem = pl.BlockSpec(memory_space=pltpu.VMEM)
     smem = pl.BlockSpec(memory_space=pltpu.SMEM)
+    far = pl.BlockSpec(memory_space=pltpu.HBM)
     return pl.pallas_call(
         kernel,
-        in_specs=[smem] * n_scalar + [vmem] * n_vector,
+        in_specs=[smem] * n_scalar + [far] * n_far + [vmem] * n_vector,
         out_specs=[vmem] * len(outs),
         out_shape=[jax.ShapeDtypeStruct(shape, F32) for shape in outs],
-        scratch_shapes=[pltpu.VMEM(shape, dtype) for shape, dtype in scratch],
-        compiler_params=pltpu.CompilerParams(vmem_limit_bytes=48 * 1024 * 1024),
+        scratch_shapes=list(scratch),
+        compiler_params=pltpu.CompilerParams(vmem_limit_bytes=mib * 1024 * 1024),
     )
 
 
@@ -362,31 +423,41 @@
     def swap(value):
         return lax.ppermute(value, "mesh", [(i, i ^ 1) for i in range(count)])
 
+    stay = functools.partial(pltpu.with_memory_space_constraint, memory_space=pltpu.HBM)
+    slots = tile_values.shape[0]
+    index = pltpu.SMEM((slots,), jnp.int32)
+    lines = pltpu.VMEM((rowb, BLK), F32)
+    tiles = pltpu.VMEM(tile_values.shape, BF16)
+    acc = pltpu.VMEM((rowb + HB, BLK, BLK), F32)
+    pieces = pltpu.VMEM((rowb + HB, 2 * BLK, BLK), BF16)
     field, part, ahead, behind = call(
-        first_kernel, 4, 3,
+        first_kernel, 2, 5, 0,
         [(nodes, width), (nodes, width), (2 * head + 8, width), (head, width)],
-        [((rowb + HB, BLK, BLK), F32), ((rowb + HB, 2 * BLK, BLK), BF16)],
-    )(tile_rows, tile_offsets, tile_count, node_count, rhs, diag, tile_values)
+        [
+            acc, pieces, index, index, pltpu.VMEM((nodes, width), F32), lines, tiles,
+            pltpu.SemaphoreType.DMA((5,)),
+        ],
+    )(tile_count, node_count, *map(stay, (tile_rows, tile_offsets, rhs, diag, tile_values)))
     from_ahead = lax.ppermute(ahead, "mesh", [(i + 1, i) for i in range(count - 1)])
     from_behind = lax.ppermute(behind, "mesh", [(i, i + 1) for i in range(count - 1)])
     image, keep, give = call(
-        second_kernel, 5, 7,
+        second_kernel, 3, 4, 5,
         [(nodes, width), (BLK + 8, BLK), (BLK + 8, BLK)],
         [
-            ((rowb + HB, BLK, BLK), F32), ((rowb + HB, 2 * BLK, BLK), BF16),
-            ((nodes, 2 * BLK), BF16), ((nodes, 2 * BLK), BF16),
-            ((nodes, BLK), BF16), ((nodes, BLK), BF16),
+            acc, pieces, pltpu.VMEM((nodes, 2 * BLK), BF16), pltpu.VMEM((nodes, 2 * BLK), BF16),
+            pltpu.VMEM((nodes, BLK), BF16), pltpu.VMEM((nodes, BLK), BF16),
+            index, index, lines, tiles, pltpu.SemaphoreType.DMA((4,)),
         ],
-    )(tile_rows, tile_offsets, tile_count, node_count, core,
-      field, part, diag, tile_values, behind, from_behind, from_ahead)
+    )(tile_count, node_count, core, *map(stay, (tile_rows, tile_offsets, diag, tile_values)),
+      field, part, behind, from_behind, from_ahead)
     total = keep + swap(give)
     total = total + functools.reduce(jnp.add, [moved(total, d, 0) for d in range(1, nx)])
     total = total + functools.reduce(jnp.add, [moved(total, 0, d) for d in range(1, ny)])
-    (coef,) = call(solve_kernel, 1, 2, [(2 * BLK, BLK)])(core, total, swap(total))
+    (coef,) = call(solve_kernel, 1, 0, 2, [(2 * BLK, BLK)])(core, total, swap(total))
     solution, keep, give = call(
-        third_kernel, 3, 4,
+        third_kernel, 3, 0, 4,
         [(nodes, width), (lead_half, BLK, BLK), (lead_half, BLK, BLK)],
-        [((rowb, 2 * BLK, BLK), BF16)],
+        [pltpu.VMEM((rowb, 2 * BLK, BLK), BF16)],
     )(inc_rows, inc_blocks, core, field, image, coef, inc_values)
     half = (keep + swap(give)).reshape(nx * ny, SRCB_DEV * BLK, width)
     groups = [[2 * i + c for i in range(nx * ny)] for c in range(2)]

time: 151 us -> 124 us (0.82); the launches traced: 150 us -> 125 us
  Pallas kernels: 54.6 us -> 37.8 us
  local copies, waits for them, and re-layouts: 8.34 us -> 0.68 us
    pallas_call x4, Pallas kernels: 54.6 us -> 37.8 us  [the longest x1 11.2 us: body(): call(solve_kernel, 1, 0, 2, [(2 * BLK, BLK)])(core, total, swap(total))]
    unnamed x28 -> x6, local copies, waits for them, and re-layouts: 7.68 us -> 0.01 us
  transfers between devices with their start and end apart: 11 -> 11, of which waited for: 8 -> 9; matrix products, arithmetic and copies ran while one was open for 0% -> 0% of each run, Pallas kernels for 0% -> 0%
where the time goes in v2:
time: 124 us; the launch traced here: 125 us
  blocking collectives  49.5 us (40%)
  Pallas kernels  37.8 us (30%)
  waiting for transfers between devices  18.9 us (15%)
  starting transfers between devices  15.4 us (12%)
  between operations  2.05 us (2%)
    all_to_all x1, blocking collectives, body(): lax.all_to_all(half, 'mesh', split_axis=0, concat_axis=0, tiled=True, axi...  32.2 us
    all_to_all x1, blocking collectives, body(): lax.all_to_all(got.sum(0), 'elec', split_axis=0, concat_axis=1, tiled=True)  17.3 us
    pallas_call x1, Pallas kernels, body(): call(solve_kernel, 1, 0, 2, [(2 * BLK, BLK)])(core, total, swap(total))  11.2 us
    ppermute x6, starting transfers between devices, moved(): lax.ppermute(value, 'mesh', [(place(x, y, c), place(x + dx, y + dy, c)) f...  10.6 us
    pallas_call x1, Pallas kernels, body(): call(second_kernel, 3, 4, 5, [(nodes, width), (BLK + 8, BLK), (BLK + 8, B...  9.87 us
    pallas_call x1, Pallas kernels, body(): call(first_kernel, 2, 5, 0, [(nodes, width), (nodes, width), (2 * head +...  8.46 us
    pallas_call x1, Pallas kernels, body(): call(third_kernel, 3, 0, 4, [(nodes, width), (lead_half, BLK, BLK), (lead...  8.31 us
    ppermute x6, waiting for transfers between devices, moved(): lax.ppermute(value, 'mesh', [(place(x, y, c), place(x + dx, y + dy, c)) f...  8.29 us
  transfers between devices with their start and end apart: 11, of which 9 were waited for; matrix products, arithmetic and copies ran while one was open for 0% of the time, Pallas kernels for 0%

profile of v2, /device:TPU:8, one launch (start us, length us, event | category | flops | bytes accessed | tf_op | source)
XLA Modules:
  0.0 124.9 jit_solution(2467034611584970057)
XLA Ops:
  1.9 8.5 %shard_map.113 = (f32[2048,128]{1,0:T(8,128)S(1)}, f32[2048,128]{1,0:T(8,128)S(1)}, f32[520,128]{1,0:T(8,128)S(1)}, f32[256,128]{1,0:T(8,128)S(1)}) custom-call(s32[1]{0:T(128)S(6)} %copy.15.tcount, s32[1]{0:T(128)S(6)} %copy.16.ncount, s32[64]{0:T(128)} %trow_far.3, s32[64]{0:T(128)} %toff_far.3, f32[2048,128]{1,0:T(8,128)} %rhs_far.1, f32[16,128]{1,0:T(8,128)} %bitcast.12, ...), custom_call_target="tpu_custom_call" | custom-call | tf_op jit(solution)/shard_map/pallas_call | solution.py:433
  10.4 1.9 %collective-permute-start.1 = (f32[520,128]{1,0:T(8,128)S(1)}, f32[520,128]{1,0:T(8,128)S(1)}, u32[]{:S(2)}, u32[]{:S(2)}) collective-permute-start(f32[520,128]{1,0:T(8,128)S(1)} %get-tuple-element.15), channel_id=1, source_target_pairs={{8,0},{16,8},{24,16},{32,24},{40,32},{48,40},{56,48},{64,56},{72,6... | collective-permute-start | bytes 798728 | tf_op jit(solution)/shard_map/ppermute | solution.py:441
  12.3 2.4 %collective-permute-start = (f32[256,128]{1,0:T(8,128)S(1)}, f32[256,128]{1,0:T(8,128)S(1)}, u32[]{:S(2)}, u32[]{:S(2)}) collective-permute-start(f32[256,128]{1,0:T(8,128)S(1)} %get-tuple-element.14.behind), channel_id=1, source_target_pairs={{0,8},{8,16},{16,24},{24,32},{32,40},{40,48},{48,56},{56,64},{64,7... | collective-permute-start | bytes 393224 | tf_op jit(solution)/shard_map/ppermute | solution.py:442
  14.7 4.1 %collective-permute-done.from_behind = f32[256,128]{1,0:T(8,128)S(1)} collective-permute-done((f32[256,128]{1,0:T(8,128)S(1)}, f32[256,128]{1,0:T(8,128)S(1)}, u32[]{:S(2)}, u32[]{:S(2)}) %collective-permute-start) | collective-permute-done | bytes 131104 | tf_op jit(solution)/shard_map/ppermute | solution.py:442
  18.8 0.0 collective-permute-done.1.from_ahead
  18.8 0.0 copy-start
  18.8 0.0 copy-start.1
  18.8 0.0 copy-start.2
  18.8 9.9 %shard_map.114 = (f32[2048,128]{1,0:T(8,128)S(1)}, f32[136,128]{1,0:T(8,128)S(1)}, f32[136,128]{1,0:T(8,128)S(1)}) custom-call(s32[1]{0:T(128)S(6)} %copy.15.tcount, s32[1]{0:T(128)S(6)} %copy.16.ncount, s32[1]{0:T(128)} %bitcast.core, s32[64]{0:T(128)} %trow_far.3, s32[64]{0:T(128)} %toff_far.3, f32[16,128]{1,0:T(8,128)} %bitcast.13, ...), custom_call_target="tpu_custom_call" | custom-call | tf_op jit(solution)/shard_map/pallas_call | solution.py:443
  28.7 0.1 collective-permute-start.2
  28.8 1.2 collective-permute-done.2
  30.1 0.1 collective-permute-start.5
  30.2 1.8 %collective-permute-start.4 = (f32[136,128]{1,0:T(8,128)S(1)}, f32[136,128]{1,0:T(8,128)S(1)}, u32[]{:S(2)}, u32[]{:S(2)}) collective-permute-start(f32[136,128]{1,0:T(8,128)S(1)} %add.29), channel_id=1, source_target_pairs={{0,128},{8,136},{16,144},{24,152},{32,160},{40,168},{48,176},{56,1... | collective-permute-start | bytes 208904 | tf_op jit(solution)/shard_map/ppermute | solution.py:418
  31.9 1.3 %collective-permute-start.3 = (f32[136,128]{1,0:T(8,128)S(1)}, f32[136,128]{1,0:T(8,128)S(1)}, u32[]{:S(2)}, u32[]{:S(2)}) collective-permute-start(f32[136,128]{1,0:T(8,128)S(1)} %add.29), channel_id=1, source_target_pairs={{0,64},{8,72},{16,80},{24,88},{32,96},{40,104},{48,112},{56,120},{... | collective-permute-start | bytes 208904 | tf_op jit(solution)/shard_map/ppermute | solution.py:418
  33.3 1.8 %collective-permute-done.5 = f32[136,128]{1,0:T(8,128)S(1)} collective-permute-done((f32[136,128]{1,0:T(8,128)S(1)}, f32[136,128]{1,0:T(8,128)S(1)}, u32[]{:S(2)}, u32[]{:S(2)}) %collective-permute-start.5) | collective-permute-done | bytes 69664 | tf_op jit(solution)/shard_map/ppermute | solution.py:418
  35.0 1.1 collective-permute-done.4
  36.1 1.5 %collective-permute-done.3 = f32[136,128]{1,0:T(8,128)S(1)} collective-permute-done((f32[136,128]{1,0:T(8,128)S(1)}, f32[136,128]{1,0:T(8,128)S(1)}, u32[]{:S(2)}, u32[]{:S(2)}) %collective-permute-start.3) | collective-permute-done | bytes 69664 | tf_op jit(solution)/shard_map/ppermute | solution.py:418
  37.6 5.6 %collective-permute-start.8 = (f32[136,128]{1,0:T(8,128)S(1)}, f32[136,128]{1,0:T(8,128)S(1)}, u32[]{:S(2)}, u32[]{:S(2)}) collective-permute-start(f32[136,128]{1,0:T(8,128)S(1)} %add_add_fusion.1), channel_id=1, source_target_pairs={{0,48},{8,56},{16,0},{24,8},{32,16},{40,24},{48,32},{56,40},{64,11... | collective-permute-start | bytes 208904 | tf_op jit(solution)/shard_map/ppermute | solution.py:418
  43.2 0.0 collective-permute-start.7
  43.2 1.8 %collective-permute-start.6 = (f32[136,128]{1,0:T(8,128)S(1)}, f32[136,128]{1,0:T(8,128)S(1)}, u32[]{:S(2)}, u32[]{:S(2)}) collective-permute-start(f32[136,128]{1,0:T(8,128)S(1)} %add_add_fusion.1), channel_id=1, source_target_pairs={{0,16},{8,24},{16,32},{24,40},{32,48},{40,56},{48,0},{56,8},{64,80... | collective-permute-start | bytes 208904 | tf_op jit(solution)/shard_map/ppermute | solution.py:418
  45.0 0.2 collective-permute-done.8
  45.2 3.7 %collective-permute-done.7 = f32[136,128]{1,0:T(8,128)S(1)} collective-permute-done((f32[136,128]{1,0:T(8,128)S(1)}, f32[136,128]{1,0:T(8,128)S(1)}, u32[]{:S(2)}, u32[]{:S(2)}) %collective-permute-start.7) | collective-permute-done | bytes 69664 | tf_op jit(solution)/shard_map/ppermute | solution.py:418
  49.0 0.0 collective-permute-done.6
  49.0 0.3 collective-permute-start.9
  49.3 1.2 collective-permute-done.9.other
  50.5 11.2 %shard_map.115.coef = f32[256,128]{1,0:T(8,128)S(1)} custom-call(s32[1]{0:T(128)} %bitcast.core, f32[136,128]{1,0:T(8,128)S(1)} %add_add_fusion.mine, f32[136,128]{1,0:T(8,128)S(1)} %collective-permute-done.9.other), custom_call_target="tpu_custom_call" | custom-call | tf_op jit(solution)/shard_map/pallas_call | solution.py:456
  61.7 0.0 copy-done
  61.8 0.0 copy-done.1
  61.8 0.0 copy-done.2
  61.8 8.3 %shard_map.116 = (f32[2048,128]{1,0:T(8,128)}, f32[32,128,128]{2,1,0:T(8,128)S(1)}, f32[32,128,128]{2,1,0:T(8,128)S(1)}) custom-call(s32[16]{0:T(128)S(1)} %copy-done.1, s32[16]{0:T(128)S(1)} %copy-done.2, s32[1]{0:T(128)} %bitcast.core, f32[2048,128]{1,0:T(8,128)S(1)} %get-tuple-element.12.field, f32[2048,128]{1,0:T(8,128)S(1)} %get-tuple-element.16.image, ...), custom_call_target="tpu_custom_call" | custom-call | tf_op jit(solution)/shard_map/pallas_call | solution.py:457
  70.1 0.2 collective-permute-start.10
  70.2 4.0 %collective-permute-done.10 = f32[32,128,128]{2,1,0:T(8,128)S(1)} collective-permute-done((f32[32,128,128]{2,1,0:T(8,128)S(1)}, f32[32,128,128]{2,1,0:T(8,128)S(1)}, u32[]{:S(2)}, u32[]{:S(2)}) %collective-permute-start.10) | collective-permute-done | bytes 2097184 | tf_op jit(solution)/shard_map/ppermute | solution.py:424
  74.2 0.3 add.36
  74.6 32.2 %all_to_all.24 = f32[16,256,128]{2,1,0:T(8,128)S(1)} all-to-all(f32[16,256,128]{2,1,0:T(8,128)S(1)} %bitcast.10), channel_id=1, replica_groups={{0,16,32,48,64,80,96,112,128,144,160,176,192,208,224,240},{8,24,40,56,7..., dimensions={0} | all-to-all | bytes 4194304 | tf_op jit(solution)/shard_map/all_to_all | solution.py:464
  106.8 0.1 reduce_sum.9
  106.9 17.3 %all_to_all.25 = f32[8,32,128]{2,1,0:T(8,128)S(1)} all-to-all(f32[8,32,128]{2,1,0:T(8,128)S(1)} %bitcast.11), channel_id=1, replica_groups=mesh['mesh'=32,'elec'=8] {'elec'}, dimensions={0} | all-to-all | bytes 262144 | tf_op jit(solution)/shard_map/all_to_all | solution.py:467
  124.2 0.7 copy_bitcast_fusion
  (3 shorter events, 0.1 us)
Async XLA Ops:
  10.4 8.4 %collective-permute-start.1 = (f32[520,128]{1,0:T(8,128)S(1)}, f32[520,128]{1,0:T(8,128)S(1)}, u32[]{:S(2)}, u32[]{:S(2)}) collective-permute-start(f32[520,128]{1,0:T(8,128)S(1)} %get-tuple-element.15), channel_id=1, source_target_pairs={{8,0},{16,8},{24,16},{32,24},{40,32},{48,40},{56,48},{64,56},{72,6... | collective-permute-start | bytes 798728 | tf_op jit(solution)/shard_map/ppermute | solution.py:441
  12.3 6.5 %collective-permute-start = (f32[256,128]{1,0:T(8,128)S(1)}, f32[256,128]{1,0:T(8,128)S(1)}, u32[]{:S(2)}, u32[]{:S(2)}) collective-permute-start(f32[256,128]{1,0:T(8,128)S(1)} %get-tuple-element.14.behind), channel_id=1, source_target_pairs={{0,8},{8,16},{16,24},{24,32},{32,40},{40,48},{48,56},{56,64},{64,7... | collective-permute-start | bytes 393224 | tf_op jit(solution)/shard_map/ppermute | solution.py:442
  18.8 42.9 %copy-start = (bf16[16,128,128]{2,1,0:T(8,128)(2,1)S(1)}, bf16[16,128,128]{2,1,0:T(8,128)(2,1)}, u32[]{:S(2)}) copy-start(bf16[16,128,128]{2,1,0:T(8,128)(2,1)} %inc.1) | copy-start | bytes 1572868
  18.8 42.9 %copy-start.1 = (s32[16]{0:T(128)S(1)}, s32[16]{0:T(128)}, u32[]{:S(2)}) copy-start(s32[16]{0:T(128)} %irow.1) | copy-start | bytes 196
  18.8 42.9 %copy-start.2 = (s32[16]{0:T(128)S(1)}, s32[16]{0:T(128)}, u32[]{:S(2)}) copy-start(s32[16]{0:T(128)} %iblk.1) | copy-start | bytes 196
  28.7 1.3 %collective-permute-start.2 = (f32[136,128]{1,0:T(8,128)S(1)}, f32[136,128]{1,0:T(8,128)S(1)}, u32[]{:S(2)}, u32[]{:S(2)}) collective-permute-start(f32[136,128]{1,0:T(8,128)S(1)} %get-tuple-element.18), channel_id=1, source_target_pairs={{0,8},{8,0},{16,24},{24,16},{32,40},{40,32},{48,56},{56,48},{64,72... | collective-permute-start | bytes 208904 | tf_op jit(solution)/shard_map/ppermute | solution.py:424
  30.1 5.0 %collective-permute-start.5 = (f32[136,128]{1,0:T(8,128)S(1)}, f32[136,128]{1,0:T(8,128)S(1)}, u32[]{:S(2)}, u32[]{:S(2)}) collective-permute-start(f32[136,128]{1,0:T(8,128)S(1)} %add.29), channel_id=1, source_target_pairs={{0,192},{8,200},{16,208},{24,216},{32,224},{40,232},{48,240},{56,2... | collective-permute-start | bytes 208904 | tf_op jit(solution)/shard_map/ppermute | solution.py:418
  30.2 5.9 %collective-permute-start.4 = (f32[136,128]{1,0:T(8,128)S(1)}, f32[136,128]{1,0:T(8,128)S(1)}, u32[]{:S(2)}, u32[]{:S(2)}) collective-permute-start(f32[136,128]{1,0:T(8,128)S(1)} %add.29), channel_id=1, source_target_pairs={{0,128},{8,136},{16,144},{24,152},{32,160},{40,168},{48,176},{56,1... | collective-permute-start | bytes 208904 | tf_op jit(solution)/shard_map/ppermute | solution.py:418
  31.9 5.6 %collective-permute-start.3 = (f32[136,128]{1,0:T(8,128)S(1)}, f32[136,128]{1,0:T(8,128)S(1)}, u32[]{:S(2)}, u32[]{:S(2)}) collective-permute-start(f32[136,128]{1,0:T(8,128)S(1)} %add.29), channel_id=1, source_target_pairs={{0,64},{8,72},{16,80},{24,88},{32,96},{40,104},{48,112},{56,120},{... | collective-permute-start | bytes 208904 | tf_op jit(solution)/shard_map/ppermute | solution.py:418
  37.6 7.6 %collective-permute-start.8 = (f32[136,128]{1,0:T(8,128)S(1)}, f32[136,128]{1,0:T(8,128)S(1)}, u32[]{:S(2)}, u32[]{:S(2)}) collective-permute-start(f32[136,128]{1,0:T(8,128)S(1)} %add_add_fusion.1), channel_id=1, source_target_pairs={{0,48},{8,56},{16,0},{24,8},{32,16},{40,24},{48,32},{56,40},{64,11... | collective-permute-start | bytes 208904 | tf_op jit(solution)/shard_map/ppermute | solution.py:418
  43.2 5.8 %collective-permute-start.7 = (f32[136,128]{1,0:T(8,128)S(1)}, f32[136,128]{1,0:T(8,128)S(1)}, u32[]{:S(2)}, u32[]{:S(2)}) collective-permute-start(f32[136,128]{1,0:T(8,128)S(1)} %add_add_fusion.1), channel_id=1, source_target_pairs={{0,32},{8,40},{16,48},{24,56},{32,0},{40,8},{48,16},{56,24},{64,96... | collective-permute-start | bytes 208904 | tf_op jit(solution)/shard_map/ppermute | solution.py:418
  43.2 5.8 %collective-permute-start.6 = (f32[136,128]{1,0:T(8,128)S(1)}, f32[136,128]{1,0:T(8,128)S(1)}, u32[]{:S(2)}, u32[]{:S(2)}) collective-permute-start(f32[136,128]{1,0:T(8,128)S(1)} %add_add_fusion.1), channel_id=1, source_target_pairs={{0,16},{8,24},{16,32},{24,40},{32,48},{40,56},{48,0},{56,8},{64,80... | collective-permute-start | bytes 208904 | tf_op jit(solution)/shard_map/ppermute | solution.py:418
  49.0 1.5 %collective-permute-start.9 = (f32[136,128]{1,0:T(8,128)S(1)}, f32[136,128]{1,0:T(8,128)S(1)}, u32[]{:S(2)}, u32[]{:S(2)}) collective-permute-start(f32[136,128]{1,0:T(8,128)S(1)} %add_add_fusion.mine), channel_id=1, source_target_pairs={{0,8},{8,0},{16,24},{24,16},{32,40},{40,32},{48,56},{56,48},{64,72... | collective-permute-start | bytes 208904 | tf_op jit(solution)/shard_map/ppermute | solution.py:424
  70.1 4.2 %collective-permute-start.10 = (f32[32,128,128]{2,1,0:T(8,128)S(1)}, f32[32,128,128]{2,1,0:T(8,128)S(1)}, u32[]{:S(2)}, u32[]{:S(2)}) collective-permute-start(f32[32,128,128]{2,1,0:T(8,128)S(1)} %get-tuple-element.21), channel_id=1, source_target_pairs={{0,8},{8,0},{16,24},{24,16},{32,40},{40,32},{48,56},{56,48},{64,72... | collective-permute-start | bytes 6291464 | tf_op jit(solution)/shard_map/ppermute | solution.py:424

commit v3 on v2

--- a/solution.py
+++ b/solution.py
@@ -6,6 +6,7 @@
 from jax.experimental import pallas as pl
 from jax.experimental.pallas import tpu as pltpu
 from jax.sharding import PartitionSpec as P
+
 
 HB = 2
 SRCB_DEV = 2
@@ -14,6 +15,7 @@
 F32 = jnp.float32
 BF16 = jnp.bfloat16
 HIGHEST = lax.Precision.HIGHEST
+GROUP = 4
 
 
 def mm(left, right, dims=((1,), (0,))):
@@ -39,19 +41,57 @@
     return jnp.transpose(jnp.broadcast_to(line, (BLK, BLK)))
 
 
-def tile_loop(count, unroll, one):
+def grouped(count, one):
     def group(g, carry):
-        for k in range(unroll):
-            one(g * unroll + k)
+        for add in [one(g * GROUP + k, g * GROUP + k < count) for k in range(GROUP)]:
+            for target, index, value in add:
+                target[index] += value
         return carry
 
-    lax.fori_loop(0, count // unroll, group, 0)
-
-    def rest(t, carry):
-        one(t)
+    lax.fori_loop(0, (count + GROUP - 1) // GROUP, group, 0)
+
+
+def chosen_loop(count, trow, toff, chosen, wanted, one):
+    def scan(t, n):
+        chosen[n] = t
+        r = trow[t]
+        return n + wanted(r, r + toff[t]).astype(jnp.int32)
+
+    n = lax.fori_loop(0, count, scan, 0)
+    grouped(n, lambda k, live: one(chosen[jnp.minimum(k, n - 1)], live))
+
+
+def block_loop(first, last, one):
+    steps = (last - first) // GROUP
+
+    def group(g, carry):
+        for k in range(GROUP):
+            one(first + g * GROUP + k)
         return carry
 
-    lax.fori_loop(count // unroll * unroll, count, rest, 0)
+    lax.fori_loop(0, steps, group, 0)
+    for b in range(first + steps * GROUP, last):
+        one(b)
+
+
+def block_at(b):
+    return pl.ds(pl.multiple_of(b * BLK, BLK), BLK)
+
+
+def halves(pieces, b, value):
+    high, low = split(value)
+    pieces[b, :BLK, :] = high
+    pieces[b, BLK:, :] = low
+    return high, low
+
+
+def forward(tile, piece):
+    return mm(jnp.concatenate([tile, tile], 1), piece)
+
+
+def backward(tile, piece):
+    flipped = jnp.transpose(tile)
+    return mm(jnp.concatenate([flipped, flipped], 1), piece)
 
 
 def fetch(pairs, sems):
@@ -64,9 +104,59 @@
     return copies
 
 
+def edge_kernel(
+    tcount, ncount, trow_far, toff_far, rhs_far, diag_far, tiles_far,
+    ahead, behind, acc, pieces, chosen, trow, toff, rhs, diag, tiles, sems,
+):
+    head = HB * BLK
+    nodes = rhs_far.shape[0]
+    rowb = nodes // BLK
+    low, high = slice(0, 2 * head), slice(nodes - head, nodes)
+    get_low, get_high, get_diag, get_row, get_off, get_tiles = fetch(
+        [
+            (rhs_far.at[low], rhs.at[low]), (rhs_far.at[high], rhs.at[high]), (diag_far, diag),
+            (trow_far, trow), (toff_far, toff), (tiles_far, tiles),
+        ],
+        sems,
+    )
+    live = ncount[0]
+    spare = 2 * HB
+    for copy in (get_low, get_high, get_diag):
+        copy.wait()
+    for b in [*range(2 * HB), *range(rowb - HB, rowb)]:
+        value = jnp.where(rows_of(b) < live, rhs[b * BLK : (b + 1) * BLK, :], 0.0)
+        halves(pieces, b, value)
+        if b < HB:
+            ahead[b * BLK : (b + 1) * BLK, :] = value
+            acc[b] = (column(diag[b : b + 1, :]) - SHIFT) * value
+    for b in range(HB, 2 * HB):
+        acc[b] = jnp.zeros((BLK, BLK), F32)
+    for copy in (get_row, get_off, get_tiles):
+        copy.wait()
+
+    def one(t, on):
+        r = trow[t]
+        c = r + toff[t]
+        tile = tiles[t]
+        inner = jnp.minimum(c, rowb - 1)
+        to_row = jnp.where(on & (r < HB), r, spare)
+        to_col = jnp.where(c >= rowb, c - rowb + HB, jnp.where(c < HB, c, spare))
+        return (
+            (acc, to_row, forward(tile, pieces[inner])),
+            (acc, jnp.where(on, to_col, spare), backward(tile, pieces[r])),
+        )
+
+    chosen_loop(tcount[0], trow, toff, chosen, lambda r, c: (r < HB) | (c >= rowb), one)
+    for b in range(HB):
+        at = slice(head + b * BLK, head + (b + 1) * BLK)
+        ahead[at, :] = jnp.where(rows_of(b) < live, acc[b], 0.0)
+        behind[b * BLK : (b + 1) * BLK, :] = acc[HB + b]
+    ahead[2 * head :, :] = jnp.full((8, BLK), live.astype(F32))
+
+
 def first_kernel(
     tcount, ncount, trow_far, toff_far, rhs_far, diag_far, tiles_far,
-    field, part, ahead, behind, acc, pieces, trow, toff, rhs, diag, tiles, sems,
+    field, part, acc, pieces, trow, toff, rhs, diag, tiles, sems,
 ):
     get_rhs, get_diag, get_row, get_off, get_tiles = fetch(
         [(rhs_far, rhs), (diag_far, diag), (trow_far, trow), (toff_far, toff), (tiles_far, tiles)],
@@ -76,49 +166,34 @@
     get_diag.wait()
     rowb = rhs.shape[0] // BLK
     live = ncount[0]
-
-    def prepare(b, carry):
-        at = pl.ds(pl.multiple_of(b * BLK, BLK), BLK)
-        value = jnp.where(rows_of(b) < live, rhs[at, :], 0.0)
-        field[at, :] = value
-        high, low = split(value)
-        pieces[b, :BLK, :] = high
-        pieces[b, BLK:, :] = low
+    spare = rowb
+
+    def prepare(b):
+        value = jnp.where(rows_of(b) < live, rhs[block_at(b), :], 0.0)
+        field[block_at(b), :] = value
+        halves(pieces, b, value)
         acc[b] = (column(diag[pl.ds(b, 1), :]) - SHIFT) * value
-        return carry
-
-    lax.fori_loop(0, rowb, prepare, 0)
-    for b in range(rowb, rowb + HB):
-        acc[b] = jnp.zeros((BLK, BLK), F32)
-        pieces[b] = jnp.zeros((2 * BLK, BLK), BF16)
-    get_row.wait()
-    get_off.wait()
-    get_tiles.wait()
-
-    def one(t):
+
+    block_loop(0, rowb, prepare)
+    for copy in (get_row, get_off, get_tiles):
+        copy.wait()
+
+    def one(t, on):
         r = trow[t]
         c = r + toff[t]
         tile = tiles[t]
-        flipped = jnp.transpose(tile)
-        forward = mm(jnp.concatenate([tile, tile], 1), pieces[c])
-        backward = mm(jnp.concatenate([flipped, flipped], 1), pieces[r])
-        acc[r] += forward
-        acc[c] += backward
-
-    tile_loop(tcount[0], 4, one)
-
-    def finish(b, carry):
-        at = pl.ds(pl.multiple_of(b * BLK, BLK), BLK)
-        part[at, :] = jnp.where(rows_of(b) < live, acc[b], 0.0)
-        return carry
-
-    lax.fori_loop(0, rowb, finish, 0)
-    head = HB * BLK
-    ahead[:head, :] = field[:head, :]
-    ahead[head : 2 * head, :] = part[:head, :]
-    ahead[2 * head :, :] = jnp.full((8, BLK), live.astype(F32))
-    for b in range(HB):
-        behind[b * BLK : (b + 1) * BLK, :] = acc[rowb + b]
+        inside = on & (c < rowb)
+        return (
+            (acc, jnp.where(inside, r, spare), forward(tile, pieces[jnp.minimum(c, rowb - 1)])),
+            (acc, jnp.where(inside, c, spare), backward(tile, pieces[r])),
+        )
+
+    grouped(tcount[0], one)
+
+    def finish(b):
+        part[block_at(b), :] = jnp.where(rows_of(b) < live, acc[b], 0.0)
+
+    block_loop(0, rowb, finish)
 
 
 def pack(first, second):
@@ -140,7 +215,7 @@
 def second_kernel(
     tcount, ncount, core,
     trow_far, toff_far, diag_far, tiles_far, field, part, behind, from_behind, from_ahead,
-    image, keep, give, acc, pieces, wide_h, wide_l, u_h, u_l, trow, toff, diag, tiles, sems,
+    wide_h, wide_l, keep, give, acc, pieces, u_h, u_l, chosen, trow, toff, diag, tiles, sems,
 ):
     get_row, get_off, get_diag, get_tiles = fetch(
         [(trow_far, trow), (toff_far, toff), (diag_far, diag), (tiles_far, tiles)], sems
@@ -150,48 +225,35 @@
     count = tcount[0]
     head = HB * BLK
     edge = rowb - HB
+    spare = rowb
 
     for b in range(HB):
-        high, low = split(from_ahead[b * BLK : (b + 1) * BLK, :])
-        pieces[rowb + b, :BLK, :] = high
-        pieces[rowb + b, BLK:, :] = low
+        halves(pieces, rowb + b, from_ahead[b * BLK : (b + 1) * BLK, :])
         acc[edge + b] = jnp.zeros((BLK, BLK), F32)
 
     for copy in (get_row, get_off, get_diag, get_tiles):
         copy.wait()
 
-    def reach(t, carry):
+    def reach(t, on):
         r = trow[t]
-        c = r + toff[t]
-
-        @pl.when(c >= rowb)
-        def _():
-            tile = tiles[t]
-            acc[r] += mm(jnp.concatenate([tile, tile], 1), pieces[c])
-
-        return carry
-
-    lax.fori_loop(0, count, reach, 0)
+        value = forward(tiles[t], pieces[r + toff[t]])
+        return ((acc, jnp.where(on, r, spare), value),)
+
+    chosen_loop(count, trow, toff, chosen, lambda r, c: c >= rowb, reach)
 
     count_ahead = from_ahead[2 * head : 2 * head + 1, :]
     for b in range(HB):
         at = slice(b * BLK, (b + 1) * BLK)
         row = rows_of(b).astype(F32)
         value = from_ahead[head + b * BLK : head + (b + 1) * BLK, :]
-        value = value + jnp.where(row < count_ahead, behind[at, :], 0.0)
-        high, low = split(value)
-        pieces[rowb + b, :BLK, :] = high
-        pieces[rowb + b, BLK:, :] = low
-
-    def settle(b, extra):
-        at = pl.ds(pl.multiple_of(b * BLK, BLK), BLK)
+        halves(pieces, rowb + b, value + jnp.where(row < count_ahead, behind[at, :], 0.0))
+
+    def settle(b, extra=None):
+        at = block_at(b)
         value = part[at, :]
         if extra is not None:
             value = value + jnp.where(rows_of(b) < live, extra, 0.0)
-        image[at, :] = value
-        high, low = split(value)
-        pieces[b, :BLK, :] = high
-        pieces[b, BLK:, :] = low
+        high, low = halves(pieces, b, value)
         wide_h[at, BLK:] = high
         wide_l[at, BLK:] = low
         high, low = split(field[at, :])
@@ -203,28 +265,21 @@
         settle(b, from_behind[b * BLK : (b + 1) * BLK, :])
     for b in range(edge, rowb):
         settle(b, acc[b])
-
-    def middle(b, carry):
-        settle(b, None)
-        return carry
-
-    lax.fori_loop(HB, edge, middle, 0)
-
-    def one(t):
+    block_loop(HB, edge, settle)
+
+    def one(t, on):
         r = trow[t]
-        tile = tiles[t]
-        acc[r] += mm(jnp.concatenate([tile, tile], 1), pieces[r + toff[t]])
-
-    tile_loop(count, 4, one)
-
-    def widen(b, carry):
-        at = pl.ds(pl.multiple_of(b * BLK, BLK), BLK)
+        value = forward(tiles[t], pieces[r + toff[t]])
+        return ((acc, jnp.where(on, r, spare), value),)
+
+    grouped(count, one)
+
+    def widen(b):
         high, low = split(acc[b])
-        u_h[at, :] = high
-        u_l[at, :] = low
-        return carry
-
-    lax.fori_loop(0, rowb, widen, 0)
+        u_h[block_at(b), :] = high
+        u_l[block_at(b), :] = low
+
+    block_loop(0, rowb, widen)
 
     first = ((0,), (0,))
     straight = mm(wide_h[...], wide_h[...], first)
@@ -268,6 +323,21 @@
                 else:
                     entry[i, j] = entry[i, j] - new[i] * old[j]
     return entry
+
+
+def thirds(value):
+    high = value.astype(BF16).astype(F32)
+    rest = value - high
+    middle = rest.astype(BF16).astype(F32)
+    return high, middle, rest - middle
+
+
+def stacked(left, right):
+    lh, lm, ll = thirds(left)
+    rh, rm, rl = thirds(right)
+    lefts = jnp.concatenate([lh, lh, lh, lm, lm, ll], 0).astype(BF16)
+    rights = jnp.concatenate([rh, rm, rl, rh, rm, rh], 0).astype(BF16)
+    return mm(lefts, rights, ((0,), (0,)))
 
 
 def invert(matrix):
@@ -307,7 +377,7 @@
             for j in range(step):
                 factor = jnp.broadcast_to(ahead[:, base + j : base + j + 1], (step, n))
                 panel = panel - factor * rows[j : j + 1, :]
-        matrix = cleared - mmh(outer, rows, ((0,), (0,)))
+        matrix = cleared - stacked(outer, rows)
         pieces = []
         if base:
             pieces.append(matrix[:base, :])
@@ -339,49 +409,49 @@
     out[BLK:, :] = y1
 
 
-def third_kernel(irow, iblk, core, field, image, coef, inc, sol, keep, give, pieces):
-    rowb = field.shape[0] // BLK
-    y0h, y0l = split(coef[:BLK, :])
-    y1h, y1l = split(coef[BLK:, :])
-    stack_h = jnp.concatenate([y0h, y1h], 0)
-    stack_l = jnp.concatenate([y0l, y1l], 0)
+def gather_kernel(irow, wide_h, wide_l, inc, out_h, out_l):
+    for u in range(inc.shape[0]):
+        at = block_at(irow[u])
+        value = backward(inc[u], jnp.concatenate([wide_h[at, :], wide_l[at, :]], 0))
+        high, low = split(value)
+        out_h[u * BLK : (u + 1) * BLK, :] = high
+        out_l[u * BLK : (u + 1) * BLK, :] = low
+
+
+def combine(left_h, left_l, coef):
+    high, low = split(coef)
+    return mm(left_h, high) + (mm(left_h, low) + mm(left_l, high))
+
+
+def scatter_kernel(iblk, core, left_h, left_l, coef, keep, give):
     keep[...] = jnp.zeros(keep.shape, F32)
     give[...] = jnp.zeros(give.shape, F32)
-
-    def combine(b, carry):
-        at = pl.ds(pl.multiple_of(b * BLK, BLK), BLK)
-        fh, fl = split(field[at, :])
-        ih, il = split(image[at, :])
-        left_h = jnp.concatenate([fh, ih], 1)
-        left_l = jnp.concatenate([fl, il], 1)
-        value = mm(left_h, stack_h) + (mm(left_h, stack_l) + mm(left_l, stack_h))
-        sol[at, :] = value
-        high, low = split(value)
-        pieces[b, :BLK, :] = high
-        pieces[b, BLK:, :] = low
-        return carry
-
-    lax.fori_loop(0, rowb, combine, 0)
-
-    def add(u, carry):
-        flipped = jnp.transpose(inc[u])
-        product = mm(jnp.concatenate([flipped, flipped], 1), pieces[irow[u]])
-        block = iblk[u]
-        owner = block // SRCB_DEV
-        at = owner // 2 * SRCB_DEV + block % SRCB_DEV
-        mine = owner % 2 == core[0]
-
-        @pl.when(mine)
-        def _():
-            keep[at] += product
-
-        @pl.when(jnp.logical_not(mine))
-        def _():
-            give[at] += product
-
-        return carry
-
-    lax.fori_loop(0, inc.shape[0], add, 0)
+    weights = coef[...]
+    for g in range(left_h.shape[0] // (GROUP * BLK)):
+        at = slice(g * GROUP * BLK, (g + 1) * GROUP * BLK)
+        product = combine(left_h[at, :], left_l[at, :], weights)
+        for k in range(GROUP):
+            value = product[k * BLK : (k + 1) * BLK, :]
+            block = iblk[g * GROUP + k]
+            owner = block // SRCB_DEV
+            to = owner // 2 * SRCB_DEV + block % SRCB_DEV
+            mine = owner % 2 == core[0]
+
+            @pl.when(mine)
+            def _():
+                keep[to] += value
+
+            @pl.when(jnp.logical_not(mine))
+            def _():
+                give[to] += value
+
+
+def third_kernel(left_h, left_l, coef, sol):
+    weights = coef[...]
+    step = GROUP * BLK
+    for g in range(sol.shape[0] // step):
+        at = slice(g * step, (g + 1) * step)
+        sol[at, :] = combine(left_h[at, :], left_l[at, :], weights)
 
 
 def call(kernel, n_scalar, n_far, n_vector, outs, scratch=(), mib=16):
@@ -392,7 +462,7 @@
         kernel,
         in_specs=[smem] * n_scalar + [far] * n_far + [vmem] * n_vector,
         out_specs=[vmem] * len(outs),
-        out_shape=[jax.ShapeDtypeStruct(shape, F32) for shape in outs],
+        out_shape=[jax.ShapeDtypeStruct(shape, (list(kind) or [F32])[0]) for shape, *kind in outs],
         scratch_shapes=list(scratch),
         compiler_params=pltpu.CompilerParams(vmem_limit_bytes=mib * 1024 * 1024),
     )
@@ -428,38 +498,50 @@
     index = pltpu.SMEM((slots,), jnp.int32)
     lines = pltpu.VMEM((rowb, BLK), F32)
     tiles = pltpu.VMEM(tile_values.shape, BF16)
-    acc = pltpu.VMEM((rowb + HB, BLK, BLK), F32)
+    acc = pltpu.VMEM((rowb + 1, BLK, BLK), F32)
     pieces = pltpu.VMEM((rowb + HB, 2 * BLK, BLK), BF16)
-    field, part, ahead, behind = call(
-        first_kernel, 2, 5, 0,
-        [(nodes, width), (nodes, width), (2 * head + 8, width), (head, width)],
+    chosen = index
+    tile_args = (tile_count, node_count, *map(stay, (tile_rows, tile_offsets, rhs, diag, tile_values)))
+    held = [index, index, pltpu.VMEM((nodes, width), F32), lines, tiles]
+    ahead, behind = call(
+        edge_kernel, 2, 5, 0,
+        [((2 * head + 8, width),), ((head, width),)],
         [
-            acc, pieces, index, index, pltpu.VMEM((nodes, width), F32), lines, tiles,
-            pltpu.SemaphoreType.DMA((5,)),
+            pltpu.VMEM((2 * HB + 1, BLK, BLK), F32), pieces, chosen, *held,
+            pltpu.SemaphoreType.DMA((6,)),
         ],
-    )(tile_count, node_count, *map(stay, (tile_rows, tile_offsets, rhs, diag, tile_values)))
+    )(*tile_args)
     from_ahead = lax.ppermute(ahead, "mesh", [(i + 1, i) for i in range(count - 1)])
     from_behind = lax.ppermute(behind, "mesh", [(i, i + 1) for i in range(count - 1)])
-    image, keep, give = call(
+    field, part = call(
+        first_kernel, 2, 5, 0,
+        [((nodes, width),), ((nodes, width),)],
+        [acc, pieces, *held, pltpu.SemaphoreType.DMA((5,))],
+    )(*tile_args)
+    wide_h, wide_l, keep, give = call(
         second_kernel, 3, 4, 5,
-        [(nodes, width), (BLK + 8, BLK), (BLK + 8, BLK)],
+        [((nodes, 2 * BLK), BF16), ((nodes, 2 * BLK), BF16), ((BLK + 8, BLK),), ((BLK + 8, BLK),)],
         [
-            acc, pieces, pltpu.VMEM((nodes, 2 * BLK), BF16), pltpu.VMEM((nodes, 2 * BLK), BF16),
-            pltpu.VMEM((nodes, BLK), BF16), pltpu.VMEM((nodes, BLK), BF16),
-            index, index, lines, tiles, pltpu.SemaphoreType.DMA((4,)),
+            acc, pieces, pltpu.VMEM((nodes, BLK), BF16), pltpu.VMEM((nodes, BLK), BF16),
+            chosen, index, index, lines, tiles, pltpu.SemaphoreType.DMA((4,)),
         ],
     )(tile_count, node_count, core, *map(stay, (tile_rows, tile_offsets, diag, tile_values)),
       field, part, behind, from_behind, from_ahead)
     total = keep + swap(give)
     total = total + functools.reduce(jnp.add, [moved(total, d, 0) for d in range(1, nx)])
     total = total + functools.reduce(jnp.add, [moved(total, 0, d) for d in range(1, ny)])
-    (coef,) = call(solve_kernel, 1, 0, 2, [(2 * BLK, BLK)])(core, total, swap(total))
-    solution, keep, give = call(
-        third_kernel, 3, 0, 4,
-        [(nodes, width), (lead_half, BLK, BLK), (lead_half, BLK, BLK)],
-        [pltpu.VMEM((rowb, 2 * BLK, BLK), BF16)],
-    )(inc_rows, inc_blocks, core, field, image, coef, inc_values)
-    half = (keep + swap(give)).reshape(nx * ny, SRCB_DEV * BLK, width)
+    other = swap(total)
+    rows = inc_values.shape[0] * BLK
+    gather_h, gather_l = call(
+        gather_kernel, 1, 0, 3, [((rows, 2 * BLK), BF16), ((rows, 2 * BLK), BF16)]
+    )(inc_rows, wide_h, wide_l, inc_values)
+    (coef,) = call(solve_kernel, 1, 0, 2, [((2 * BLK, BLK),)])(core, total, other)
+    keep, give = call(scatter_kernel, 2, 0, 3, [((lead_half, BLK, BLK),)] * 2)(
+        inc_blocks, core, gather_h, gather_l, coef
+    )
+    other = swap(give)
+    (solution,) = call(third_kernel, 0, 0, 3, [((nodes, width),)])(wide_h, wide_l, coef)
+    half = (keep + other).reshape(nx * ny, SRCB_DEV * BLK, width)
     groups = [[2 * i + c for i in range(nx * ny)] for c in range(2)]
     got = lax.all_to_all(
         half, "mesh", split_axis=0, concat_axis=0, tiled=True, axis_index_groups=groups
@@ -481,8 +563,12 @@
         P("mesh"),
         P("mesh"),
     )
+
+    def whole(*args):
+        return body((4, 4), *args)
+
     return jax.shard_map(
-        functools.partial(body, (4, 4)),
+        whole,
         mesh=mesh,
         in_specs=placed,
         out_specs=(P("mesh", "elec"), P(("mesh", "elec"), None)),

time: 124 us -> 122 us (0.984); the launches traced: 125 us -> 121 us
  blocking collectives: 49.5 us -> 34 us
  starting transfers between devices: 15.4 us -> 30.3 us
  Pallas kernels: 37.8 us -> 28.3 us
  local copies, waits for them, and re-layouts: 0.68 us -> 4.43 us
  other arithmetic: 0.49 us -> 2.74 us
    all_to_all x1 -> x0, blocking collectives: 17.3 us -> none  [body(): lax.all_to_all(got.sum(0), 'elec', split_axis=0, concat_axis=1, tiled=True)]
    pallas_call x4 -> x7, Pallas kernels: 37.8 us -> 28.3 us  [the longest x1 9.47 us: body(): coef, = call(solve_kernel, 1, 0, 2, [((2 * BLK, BLK),)])(core, total, other)]
    all_to_all x0 -> x1, starting transfers between devices: none -> 8.47 us  [body(): lax.all_to_all(got.sum(0), 'elec', split_axis=0, concat_axis=1, tiled=True)]
    all_to_all x0 -> x1, waiting for transfers between devices: none -> 7.13 us  [body(): lax.all_to_all(got.sum(0), 'elec', split_axis=0, concat_axis=1, tiled=True)]
    ppermute x3, starting transfers between devices: 0.52 us -> 6.52 us  [swap(): return lax.ppermute(value, 'mesh', [(i, i ^ 1) for i in range(count)])]
    ppermute x1, waiting for transfers between devices: 4.09 us -> 0.01 us  [body(): lax.ppermute(behind, 'mesh', [(i, i + 1) for i in range(count - 1)])]
    unnamed x6 -> x14, local copies, waits for them, and re-layouts: 0.01 us -> 3.76 us
    reduce_sum x1, other arithmetic: 0.1 us -> 2.35 us  [body(): got.sum(0)]
  transfers between devices with their start and end apart: 11 -> 12, of which waited for: 9 -> 9; matrix products, arithmetic and copies ran while one was open for 0% -> 0% of each run, Pallas kernels for 0% -> 6%
where the time goes in v3:
time: 122 us; the launch traced here: 121 us
  blocking collectives  34 us (28%)
  starting transfers between devices  30.3 us (25%)
  Pallas kernels  28.3 us (23%)
  waiting for transfers between devices  19.4 us (16%)
  local copies, waits for them, and re-layouts  4.43 us (4%)
  other arithmetic  2.74 us (2%)
  between operations  2.07 us (2%)
    all_to_all x1, blocking collectives, body(): lax.all_to_all(half, 'mesh', split_axis=0, concat_axis=0, tiled=True, axi...  34 us
    ppermute x6, starting transfers between devices, moved(): lax.ppermute(value, 'mesh', [(place(x, y, c), place(x + dx, y + dy, c)) f...  11 us
    pallas_call x1, Pallas kernels, body(): coef, = call(solve_kernel, 1, 0, 2, [((2 * BLK, BLK),)])(core, total, other)  9.47 us
    all_to_all x1, starting transfers between devices, body(): lax.all_to_all(got.sum(0), 'elec', split_axis=0, concat_axis=1, tiled=True)  8.47 us
    ppermute x6, waiting for transfers between devices, moved(): lax.ppermute(value, 'mesh', [(place(x, y, c), place(x + dx, y + dy, c)) f...  7.23 us
    all_to_all x1, waiting for transfers between devices, body(): lax.all_to_all(got.sum(0), 'elec', split_axis=0, concat_axis=1, tiled=True)  7.13 us
    ppermute x3, starting transfers between devices, swap(): return lax.ppermute(value, 'mesh', [(i, i ^ 1) for i in range(count)])  6.52 us
    pallas_call x1, Pallas kernels, body(): call(second_kernel, 3, 4, 5, [((nodes, 2 * BLK), BF16), ((nodes, 2 * BLK)...  5.76 us
  transfers between devices with their start and end apart: 12, of which 9 were waited for; matrix products, arithmetic and copies ran while one was open for 0% of the time, Pallas kernels for 6%

profile of v3, /device:TPU:8, one launch (start us, length us, event | category | flops | bytes accessed | tf_op | source)
XLA Modules:
  0.0 121.2 jit_solution(11889845148352584288)
XLA Ops:
  1.9 2.2 %shard_map.114 = (f32[520,128]{1,0:T(8,128)S(1)}, f32[256,128]{1,0:T(8,128)S(1)}) custom-call(s32[1]{0:T(128)S(6)} %copy.15.tcount, s32[1]{0:T(128)S(6)} %copy.16.ncount, s32[64]{0:T(128)} %trow_far.5, s32[64]{0:T(128)} %toff_far.5, f32[2048,128]{1,0:T(8,128)} %rhs_far.3, f32[16,128]{1,0:T(8,128)} %bitcast.11, bf16[64,128,128]{2,1,0:T(8,128)(2,1)} %tiles_far.5), custom_call_target="tpu_custom_call" | custom-call | tf_op jit(solution)/shard_map/pallas_call | solution.py:506
  4.1 1.9 %collective-permute-start.1 = (f32[520,128]{1,0:T(8,128)S(1)}, f32[520,128]{1,0:T(8,128)S(1)}, u32[]{:S(2)}, u32[]{:S(2)}) collective-permute-start(f32[520,128]{1,0:T(8,128)S(1)} %get-tuple-element.17), channel_id=1, source_target_pairs={{8,0},{16,8},{24,16},{32,24},{40,32},{48,40},{56,48},{64,56},{72,6... | collective-permute-start | bytes 798728 | tf_op jit(solution)/shard_map/ppermute | solution.py:514
  6.0 2.4 %collective-permute-start = (f32[256,128]{1,0:T(8,128)S(1)}, f32[256,128]{1,0:T(8,128)S(1)}, u32[]{:S(2)}, u32[]{:S(2)}) collective-permute-start(f32[256,128]{1,0:T(8,128)S(1)} %get-tuple-element.16.behind), channel_id=1, source_target_pairs={{0,8},{8,16},{16,24},{24,32},{32,40},{40,48},{48,56},{56,64},{64,7... | collective-permute-start | bytes 393224 | tf_op jit(solution)/shard_map/ppermute | solution.py:515
  8.5 4.6 %shard_map.113 = (f32[2048,128]{1,0:T(8,128)S(1)}, f32[2048,128]{1,0:T(8,128)S(1)}) custom-call(s32[1]{0:T(128)S(6)} %copy.15.tcount, s32[1]{0:T(128)S(6)} %copy.16.ncount, s32[64]{0:T(128)} %trow_far.5, s32[64]{0:T(128)} %toff_far.5, f32[2048,128]{1,0:T(8,128)} %rhs_far.3, f32[16,128]{1,0:T(8,128)} %bitcast.12, bf16[64,128,128]{2,1,0:T(8,128)(2,1)} %tiles_far.5), custom_call_target="tpu_custom_call" | custom-call | tf_op jit(solution)/shard_map/pallas_call | solution.py:516
  13.1 0.0 copy-start
  13.1 1.0 copy-done
  14.1 0.0 collective-permute-done.from_behind
  14.1 0.0 copy-start.3
  14.1 0.7 copy-done.3
  14.7 0.0 collective-permute-done.1.from_ahead
  14.7 0.0 copy-start.1
  14.7 1.2 %copy-done.1 = f32[2048,128]{1,0:T(8,128)S(1)} copy-done((f32[2048,128]{1,0:T(8,128)S(1)}, f32[2048,128]{1,0:T(8,128)}, u32[]{:S(2)}) %copy-start.1) | copy-done | bytes 1048600
  15.9 0.0 copy-start.4
  15.9 0.9 copy-done.4
  16.8 0.0 copy-start.2
  16.8 0.0 copy-start.5
  16.8 5.8 %shard_map.115 = (bf16[2048,256]{1,0:T(8,128)(2,1)S(1)}, bf16[2048,256]{1,0:T(8,128)(2,1)S(1)}, f32[136,128]{1,0:T(8,128)S(1)}, f32[136,128]{1,0:T(8,128)S(1)}) custom-call(s32[1]{0:T(128)S(6)} %copy.15.tcount, s32[1]{0:T(128)S(6)} %copy.16.ncount, s32[1]{0:T(128)} %bitcast.core, s32[64]{0:T(128)} %trow_far.5, s32[64]{0:T(128)} %toff_far.5, ...), custom_call_target="tpu_custom_call" | custom-call | tf_op jit(solution)/shard_map/pallas_call | solution.py:521
  22.6 0.0 copy-start.6
  22.6 5.9 %collective-permute-start.2 = (f32[136,128]{1,0:T(8,128)S(1)}, f32[136,128]{1,0:T(8,128)S(1)}, u32[]{:S(2)}, u32[]{:S(2)}) collective-permute-start(f32[136,128]{1,0:T(8,128)S(1)} %get-tuple-element.21), channel_id=1, source_target_pairs={{0,8},{8,0},{16,24},{24,16},{32,40},{40,32},{48,56},{56,48},{64,72... | collective-permute-start | bytes 208904 | tf_op jit(solution)/shard_map/ppermute | solution.py:494
  28.5 0.9 collective-permute-done.2
  29.4 2.9 %collective-permute-start.5 = (f32[136,128]{1,0:T(8,128)S(1)}, f32[136,128]{1,0:T(8,128)S(1)}, u32[]{:S(2)}, u32[]{:S(2)}) collective-permute-start(f32[136,128]{1,0:T(8,128)S(1)} %add.29), channel_id=1, source_target_pairs={{0,192},{8,200},{16,208},{24,216},{32,224},{40,232},{48,240},{56,2... | collective-permute-start | bytes 208904 | tf_op jit(solution)/shard_map/ppermute | solution.py:488
  32.3 0.4 collective-permute-start.4
  32.6 1.3 %collective-permute-start.3 = (f32[136,128]{1,0:T(8,128)S(1)}, f32[136,128]{1,0:T(8,128)S(1)}, u32[]{:S(2)}, u32[]{:S(2)}) collective-permute-start(f32[136,128]{1,0:T(8,128)S(1)} %add.29), channel_id=1, source_target_pairs={{0,64},{8,72},{16,80},{24,88},{32,96},{40,104},{48,112},{56,120},{... | collective-permute-start | bytes 208904 | tf_op jit(solution)/shard_map/ppermute | solution.py:488
  34.0 1.7 %collective-permute-done.5 = f32[136,128]{1,0:T(8,128)S(1)} collective-permute-done((f32[136,128]{1,0:T(8,128)S(1)}, f32[136,128]{1,0:T(8,128)S(1)}, u32[]{:S(2)}, u32[]{:S(2)}) %collective-permute-start.5) | collective-permute-done | bytes 69664 | tf_op jit(solution)/shard_map/ppermute | solution.py:488
  35.6 2.9 %collective-permute-done.4 = f32[136,128]{1,0:T(8,128)S(1)} collective-permute-done((f32[136,128]{1,0:T(8,128)S(1)}, f32[136,128]{1,0:T(8,128)S(1)}, u32[]{:S(2)}, u32[]{:S(2)}) %collective-permute-start.4) | collective-permute-done | bytes 69664 | tf_op jit(solution)/shard_map/ppermute | solution.py:488
  38.5 0.7 collective-permute-done.3
  39.3 0.3 collective-permute-start.8
  39.6 3.6 %collective-permute-start.7 = (f32[136,128]{1,0:T(8,128)S(1)}, f32[136,128]{1,0:T(8,128)S(1)}, u32[]{:S(2)}, u32[]{:S(2)}) collective-permute-start(f32[136,128]{1,0:T(8,128)S(1)} %add_add_fusion.1), channel_id=1, source_target_pairs={{0,32},{8,40},{16,48},{24,56},{32,0},{40,8},{48,16},{56,24},{64,96... | collective-permute-start | bytes 208904 | tf_op jit(solution)/shard_map/ppermute | solution.py:488
  43.2 2.5 %collective-permute-start.6 = (f32[136,128]{1,0:T(8,128)S(1)}, f32[136,128]{1,0:T(8,128)S(1)}, u32[]{:S(2)}, u32[]{:S(2)}) collective-permute-start(f32[136,128]{1,0:T(8,128)S(1)} %add_add_fusion.1), channel_id=1, source_target_pairs={{0,16},{8,24},{16,32},{24,40},{32,48},{40,56},{48,0},{56,8},{64,80... | collective-permute-start | bytes 208904 | tf_op jit(solution)/shard_map/ppermute | solution.py:488
  45.7 0.0 collective-permute-done.8
  45.7 0.4 collective-permute-done.7
  46.1 1.5 %collective-permute-done.6 = f32[136,128]{1,0:T(8,128)S(1)} collective-permute-done((f32[136,128]{1,0:T(8,128)S(1)}, f32[136,128]{1,0:T(8,128)S(1)}, u32[]{:S(2)}, u32[]{:S(2)}) %collective-permute-start.6) | collective-permute-done | bytes 69664 | tf_op jit(solution)/shard_map/ppermute | solution.py:488
  47.7 0.3 collective-permute-start.9
  48.0 0.0 copy-done.2
  48.0 0.0 copy-done.5
  48.0 1.0 shard_map.118
  49.0 0.2 collective-permute-done.9.other
  49.2 9.5 %shard_map.116.coef = f32[256,128]{1,0:T(8,128)S(1)} custom-call(s32[1]{0:T(128)} %bitcast.core, f32[136,128]{1,0:T(8,128)S(1)} %add_add_fusion.mine, f32[136,128]{1,0:T(8,128)S(1)} %collective-permute-done.9.other), custom_call_target="tpu_custom_call" | custom-call | tf_op jit(solution)/shard_map/pallas_call | solution.py:538
  58.7 0.0 copy-done.6
  58.7 3.3 %shard_map.119 = (f32[32,128,128]{2,1,0:T(8,128)S(1)}, f32[32,128,128]{2,1,0:T(8,128)S(1)}) custom-call(s32[16]{0:T(128)S(1)} %copy-done.6, s32[1]{0:T(128)} %bitcast.core, bf16[2048,256]{1,0:T(8,128)(2,1)S(1)} %get-tuple-element.22.left_h, bf16[2048,256]{1,0:T(8,128)(2,1)S(1)} %get-tuple-element.23.left_l, f32[256,128]{1,0:T(8,128)S(1)} %shard_map.116.coef), custom_call_target="tpu_custom_call" | custom-call | tf_op jit(solution)/shard_map/pallas_call | solution.py:539
  62.1 0.4 collective-permute-start.10
  62.4 3.9 %collective-permute-done.10 = f32[32,128,128]{2,1,0:T(8,128)S(1)} collective-permute-done((f32[32,128,128]{2,1,0:T(8,128)S(1)}, f32[32,128,128]{2,1,0:T(8,128)S(1)}, u32[]{:S(2)}, u32[]{:S(2)}) %collective-permute-start.10) | collective-permute-done | bytes 2097184 | tf_op jit(solution)/shard_map/ppermute | solution.py:494
  66.3 0.3 add.36
  66.7 34.0 %all_to_all.24 = f32[16,256,128]{2,1,0:T(8,128)} all-to-all(f32[16,256,128]{2,1,0:T(8,128)S(1)} %bitcast.10), channel_id=1, replica_groups={{0,16,32,48,64,80,96,112,128,144,160,176,192,208,224,240},{8,24,40,56,7..., dimensions={0} | all-to-all | bytes 4194304 | tf_op jit(solution)/shard_map/all_to_all | solution.py:546
  100.6 2.4 %reduce_sum.9 = f32[256,128]{1,0:T(8,128)} reduce(f32[16,256,128]{2,1,0:T(8,128)} %all_to_all.24, f32[]{:T(128)} %constant.20.clone.1), dimensions={0}, to_apply=%region_0.1 | reduce | flops 491520 | bytes 2228228 | tf_op jit(solution)/shard_map/reduce_sum | solution.py:549
  103.0 8.5 %all-to-all-start.1 = ((f32[8,32,128]{2,1,0:T(8,128)}), f32[8,32,128]{2,1,0:T(8,128)S(1)}, u32[]{:S(2)}, u32[]{:S(2)}) async-start(f32[8,32,128]{2,1,0:T(8,128)} %bitcast.3), calls=%async_computation.1 | async-start | bytes 262144 | tf_op jit(solution)/shard_map/all_to_all | solution.py:549
  111.5 1.9 %shard_map.117 = f32[2048,128]{1,0:T(8,128)} custom-call(bf16[2048,256]{1,0:T(8,128)(2,1)S(1)} %get-tuple-element.18.left_h.wide_h, bf16[2048,256]{1,0:T(8,128)(2,1)S(1)} %get-tuple-element.19.left_l.wide_l, f32[256,128]{1,0:T(8,128)S(1)} %shard_map.116.coef), custom_call_target="tpu_custom_call" | custom-call | tf_op jit(solution)/shard_map/pallas_call | solution.py:543
  113.4 7.1 %all-to-all-done.1 = f32[8,32,128]{2,1,0:T(8,128)S(1)} async-done(((f32[8,32,128]{2,1,0:T(8,128)}), f32[8,32,128]{2,1,0:T(8,128)S(1)}, u32[]{:S(2)}, u32[]{:S(2)}) %all-to-all-start.1) | async-done | bytes 131104 | tf_op jit(solution)/shard_map/all_to_all | solution.py:549
  120.5 0.7 copy_bitcast_fusion
  (3 shorter events, 0.1 us)
Async XLA Ops:
  4.1 10.6 %collective-permute-start.1 = (f32[520,128]{1,0:T(8,128)S(1)}, f32[520,128]{1,0:T(8,128)S(1)}, u32[]{:S(2)}, u32[]{:S(2)}) collective-permute-start(f32[520,128]{1,0:T(8,128)S(1)} %get-tuple-element.17), channel_id=1, source_target_pairs={{8,0},{16,8},{24,16},{32,24},{40,32},{48,40},{56,48},{64,56},{72,6... | collective-permute-start | bytes 798728 | tf_op jit(solution)/shard_map/ppermute | solution.py:514
  6.0 8.0 %collective-permute-start = (f32[256,128]{1,0:T(8,128)S(1)}, f32[256,128]{1,0:T(8,128)S(1)}, u32[]{:S(2)}, u32[]{:S(2)}) collective-permute-start(f32[256,128]{1,0:T(8,128)S(1)} %get-tuple-element.16.behind), channel_id=1, source_target_pairs={{0,8},{8,16},{16,24},{24,32},{32,40},{40,48},{48,56},{56,64},{64,7... | collective-permute-start | bytes 393224 | tf_op jit(solution)/shard_map/ppermute | solution.py:515
  13.1 1.0 copy-start
  14.1 0.7 copy-start.3
  14.7 1.2 %copy-start.1 = (f32[2048,128]{1,0:T(8,128)S(1)}, f32[2048,128]{1,0:T(8,128)}, u32[]{:S(2)}) copy-start(f32[2048,128]{1,0:T(8,128)} %copy-done) | copy-start | bytes 3145732
  15.9 0.9 copy-start.4
  16.8 31.1 %copy-start.2 = (bf16[16,128,128]{2,1,0:T(8,128)(2,1)S(1)}, bf16[16,128,128]{2,1,0:T(8,128)(2,1)}, u32[]{:S(2)}) copy-start(bf16[16,128,128]{2,1,0:T(8,128)(2,1)} %inc.1) | copy-start | bytes 1572868
  16.8 31.1 %copy-start.5 = (s32[16]{0:T(128)S(1)}, s32[16]{0:T(128)}, u32[]{:S(2)}) copy-start(s32[16]{0:T(128)} %irow.1) | copy-start | bytes 196
  22.6 36.1 %copy-start.6 = (s32[16]{0:T(128)S(1)}, s32[16]{0:T(128)}, u32[]{:S(2)}) copy-start(s32[16]{0:T(128)} %iblk.1) | copy-start | bytes 196
  22.6 6.8 %collective-permute-start.2 = (f32[136,128]{1,0:T(8,128)S(1)}, f32[136,128]{1,0:T(8,128)S(1)}, u32[]{:S(2)}, u32[]{:S(2)}) collective-permute-start(f32[136,128]{1,0:T(8,128)S(1)} %get-tuple-element.21), channel_id=1, source_target_pairs={{0,8},{8,0},{16,24},{24,16},{32,40},{40,32},{48,56},{56,48},{64,72... | collective-permute-start | bytes 208904 | tf_op jit(solution)/shard_map/ppermute | solution.py:494
  29.4 6.2 %collective-permute-start.5 = (f32[136,128]{1,0:T(8,128)S(1)}, f32[136,128]{1,0:T(8,128)S(1)}, u32[]{:S(2)}, u32[]{:S(2)}) collective-permute-start(f32[136,128]{1,0:T(8,128)S(1)} %add.29), channel_id=1, source_target_pairs={{0,192},{8,200},{16,208},{24,216},{32,224},{40,232},{48,240},{56,2... | collective-permute-start | bytes 208904 | tf_op jit(solution)/shard_map/ppermute | solution.py:488
  32.3 6.2 %collective-permute-start.4 = (f32[136,128]{1,0:T(8,128)S(1)}, f32[136,128]{1,0:T(8,128)S(1)}, u32[]{:S(2)}, u32[]{:S(2)}) collective-permute-start(f32[136,128]{1,0:T(8,128)S(1)} %add.29), channel_id=1, source_target_pairs={{0,128},{8,136},{16,144},{24,152},{32,160},{40,168},{48,176},{56,1... | collective-permute-start | bytes 208904 | tf_op jit(solution)/shard_map/ppermute | solution.py:488
  32.6 6.6 %collective-permute-start.3 = (f32[136,128]{1,0:T(8,128)S(1)}, f32[136,128]{1,0:T(8,128)S(1)}, u32[]{:S(2)}, u32[]{:S(2)}) collective-permute-start(f32[136,128]{1,0:T(8,128)S(1)} %add.29), channel_id=1, source_target_pairs={{0,64},{8,72},{16,80},{24,88},{32,96},{40,104},{48,112},{56,120},{... | collective-permute-start | bytes 208904 | tf_op jit(solution)/shard_map/ppermute | solution.py:488
  39.3 6.5 %collective-permute-start.8 = (f32[136,128]{1,0:T(8,128)S(1)}, f32[136,128]{1,0:T(8,128)S(1)}, u32[]{:S(2)}, u32[]{:S(2)}) collective-permute-start(f32[136,128]{1,0:T(8,128)S(1)} %add_add_fusion.1), channel_id=1, source_target_pairs={{0,48},{8,56},{16,0},{24,8},{32,16},{40,24},{48,32},{56,40},{64,11... | collective-permute-start | bytes 208904 | tf_op jit(solution)/shard_map/ppermute | solution.py:488
  39.6 6.5 %collective-permute-start.7 = (f32[136,128]{1,0:T(8,128)S(1)}, f32[136,128]{1,0:T(8,128)S(1)}, u32[]{:S(2)}, u32[]{:S(2)}) collective-permute-start(f32[136,128]{1,0:T(8,128)S(1)} %add_add_fusion.1), channel_id=1, source_target_pairs={{0,32},{8,40},{16,48},{24,56},{32,0},{40,8},{48,16},{56,24},{64,96... | collective-permute-start | bytes 208904 | tf_op jit(solution)/shard_map/ppermute | solution.py:488
  43.2 4.5 %collective-permute-start.6 = (f32[136,128]{1,0:T(8,128)S(1)}, f32[136,128]{1,0:T(8,128)S(1)}, u32[]{:S(2)}, u32[]{:S(2)}) collective-permute-start(f32[136,128]{1,0:T(8,128)S(1)} %add_add_fusion.1), channel_id=1, source_target_pairs={{0,16},{8,24},{16,32},{24,40},{32,48},{40,56},{48,0},{56,8},{64,80... | collective-permute-start | bytes 208904 | tf_op jit(solution)/shard_map/ppermute | solution.py:488
  47.7 1.5 %collective-permute-start.9 = (f32[136,128]{1,0:T(8,128)S(1)}, f32[136,128]{1,0:T(8,128)S(1)}, u32[]{:S(2)}, u32[]{:S(2)}) collective-permute-start(f32[136,128]{1,0:T(8,128)S(1)} %add_add_fusion.mine), channel_id=1, source_target_pairs={{0,8},{8,0},{16,24},{24,16},{32,40},{40,32},{48,56},{56,48},{64,72... | collective-permute-start | bytes 208904 | tf_op jit(solution)/shard_map/ppermute | solution.py:494
  62.1 4.2 %collective-permute-start.10 = (f32[32,128,128]{2,1,0:T(8,128)S(1)}, f32[32,128,128]{2,1,0:T(8,128)S(1)}, u32[]{:S(2)}, u32[]{:S(2)}) collective-permute-start(f32[32,128,128]{2,1,0:T(8,128)S(1)} %get-tuple-element.25), channel_id=1, source_target_pairs={{0,8},{8,0},{16,24},{24,16},{32,40},{40,32},{48,56},{56,48},{64,72... | collective-permute-start | bytes 6291464 | tf_op jit(solution)/shard_map/ppermute | solution.py:494
  103.0 17.5 %all-to-all-start.1 = ((f32[8,32,128]{2,1,0:T(8,128)}), f32[8,32,128]{2,1,0:T(8,128)S(1)}, u32[]{:S(2)}, u32[]{:S(2)}) async-start(f32[8,32,128]{2,1,0:T(8,128)} %bitcast.3), calls=%async_computation.1 | async-start | bytes 262144 | tf_op jit(solution)/shard_map/all_to_all | solution.py:549

commit v4 on v3

--- a/solution.py
+++ b/solution.py
@@ -105,8 +105,8 @@
 
 
 def edge_kernel(
-    tcount, ncount, trow_far, toff_far, rhs_far, diag_far, tiles_far,
-    ahead, behind, acc, pieces, chosen, trow, toff, rhs, diag, tiles, sems,
+    tcount, ncount, core, trow_far, toff_far, rhs_far, diag_far, tiles_far,
+    behind, to_chip, to_next, ahead, acc, pieces, chosen, trow, toff, rhs, diag, tiles, sems,
 ):
     head = HB * BLK
     nodes = rhs_far.shape[0]
@@ -153,6 +153,19 @@
         behind[b * BLK : (b + 1) * BLK, :] = acc[HB + b]
     ahead[2 * head :, :] = jnp.full((8, BLK), live.astype(F32))
 
+    def place(lower, upper):
+        lower[...] = ahead[...]
+        upper[:head, :] = behind[...]
+        upper[head:, :] = jnp.zeros((head + 8, BLK), F32)
+
+    @pl.when(core[0] == 0)
+    def _():
+        place(to_next, to_chip)
+
+    @pl.when(core[0] != 0)
+    def _():
+        place(to_chip, to_next)
+
 
 def first_kernel(
     tcount, ncount, trow_far, toff_far, rhs_far, diag_far, tiles_far,
@@ -214,8 +227,8 @@
 
 def second_kernel(
     tcount, ncount, core,
-    trow_far, toff_far, diag_far, tiles_far, field, part, behind, from_behind, from_ahead,
-    wide_h, wide_l, keep, give, acc, pieces, u_h, u_l, chosen, trow, toff, diag, tiles, sems,
+    trow_far, toff_far, diag_far, tiles_far, field, part, behind, from_chip, from_next,
+    wide_h, wide_l, keep, give, acc, pieces, wide_u, chosen, trow, toff, diag, tiles, sems,
 ):
     get_row, get_off, get_diag, get_tiles = fetch(
         [(trow_far, trow), (toff_far, toff), (diag_far, diag), (tiles_far, tiles)], sems
@@ -226,6 +239,9 @@
     head = HB * BLK
     edge = rowb - HB
     spare = rowb
+    even = core[0] == 0
+    from_ahead = jnp.where(even, from_chip[...], from_next[...])
+    from_behind = jnp.where(even, from_next[:head, :], from_chip[:head, :])
 
     for b in range(HB):
         halves(pieces, rowb + b, from_ahead[b * BLK : (b + 1) * BLK, :])
@@ -276,8 +292,8 @@
 
     def widen(b):
         high, low = split(acc[b])
-        u_h[block_at(b), :] = high
-        u_l[block_at(b), :] = low
+        wide_u[block_at(b), :BLK] = high
+        wide_u[block_at(b), BLK:] = low
 
     block_loop(0, rowb, widen)
 
@@ -287,8 +303,8 @@
     n0 = straight[:BLK, :BLK] + cross[:BLK, :BLK] + jnp.transpose(cross[:BLK, :BLK])
     n1 = straight[:BLK, BLK:] + cross[:BLK, BLK:] + jnp.transpose(cross[BLK:, :BLK])
     n2 = straight[BLK:, BLK:] + cross[BLK:, BLK:] + jnp.transpose(cross[BLK:, BLK:])
-    half = mm(wide_h[:, BLK:], u_h[...], first)
-    half = half + mm(wide_h[:, BLK:], u_l[...], first) + mm(wide_l[:, BLK:], u_h[...], first)
+    both = mm(wide_h[:, BLK:], wide_u[...], first)
+    half = both[:, :BLK] + both[:, BLK:] + mm(wide_l[:, BLK:], wide_u[:, :BLK], first)
     n3 = half + jnp.transpose(half)
     n1 = 0.5 * (n1 + jnp.transpose(n1))
     low_packed, low_line = pack(n0, n1)
@@ -309,20 +325,19 @@
         place(give, keep)
 
 
-def pivot_block(entry, n):
+def pivot_block(columns):
+    n = len(columns)
+    sub = lax.broadcasted_iota(jnp.int32, columns[0].shape, 0)
     for p in range(n):
-        scale = pl.reciprocal(entry[p, p])
-        old = {i: entry[min(i, p), max(i, p)] for i in range(n) if i != p}
-        new = {i: value * scale for i, value in old.items()}
-        for i in range(n):
-            for j in range(i, n):
-                if i == p and j == p:
-                    entry[i, j] = -scale
-                elif i == p or j == p:
-                    entry[i, j] = new[i + j - p]
-                else:
-                    entry[i, j] = entry[i, j] - new[i] * old[j]
-    return entry
+        here = sub == p
+        row = [jnp.broadcast_to(value[p : p + 1, :], value.shape) for value in columns]
+        scale = pl.reciprocal(row[p])
+        factor = jnp.where(here, -scale, columns[p] * scale)
+        columns = [
+            factor if j == p else jnp.where(here, 0.0, columns[j]) - factor * row[j]
+            for j in range(n)
+        ]
+    return columns
 
 
 def thirds(value):
@@ -344,8 +359,6 @@
     n = matrix.shape[0]
     step = 8
     lane = lax.broadcasted_iota(jnp.int32, (step, n), 1)
-    sub = lax.broadcasted_iota(jnp.int32, (step, n), 0)
-    masks = [sub == i for i in range(step)]
     panel = matrix[:step, :]
     for k in range(n // step):
         base = k * step
@@ -353,21 +366,13 @@
         columns = [
             jnp.broadcast_to(panel[:, base + j : base + j + 1], (step, n)) for j in range(step)
         ]
-        entry = {
-            (i, j): jnp.broadcast_to(columns[j][i : i + 1, :], (step, n))
-            for i in range(step) for j in range(i, step)
-        }
-        entry = pivot_block(entry, step)
+        columns = pivot_block(columns)
         rows = None
-        unit = None
+        unit = columns[0]
         for j in range(step):
-            weight = entry[0, j]
-            for i in range(1, step):
-                weight = jnp.where(masks[i], entry[min(i, j), max(i, j)], weight)
-            term = weight * panel[j : j + 1, :]
+            term = columns[j] * panel[j : j + 1, :]
             rows = term if rows is None else rows + term
-            spot = jnp.where(lane == base + j, weight, 0.0)
-            unit = spot if unit is None else unit + spot
+            unit = jnp.where(lane == base + j, columns[j], unit)
         rows = jnp.where(inside, unit, -rows)
         outer = jnp.where(inside, 0.0, panel)
         cleared = jnp.where(inside[:1, :], 0.0, matrix)
@@ -503,16 +508,17 @@
     chosen = index
     tile_args = (tile_count, node_count, *map(stay, (tile_rows, tile_offsets, rhs, diag, tile_values)))
     held = [index, index, pltpu.VMEM((nodes, width), F32), lines, tiles]
-    ahead, behind = call(
-        edge_kernel, 2, 5, 0,
-        [((2 * head + 8, width),), ((head, width),)],
+    behind, to_chip, to_next = call(
+        edge_kernel, 3, 5, 0,
+        [((head, width),), ((2 * head + 8, width),), ((2 * head + 8, width),)],
         [
-            pltpu.VMEM((2 * HB + 1, BLK, BLK), F32), pieces, chosen, *held,
-            pltpu.SemaphoreType.DMA((6,)),
+            pltpu.VMEM((2 * head + 8, width), F32), pltpu.VMEM((2 * HB + 1, BLK, BLK), F32),
+            pieces, chosen, *held, pltpu.SemaphoreType.DMA((6,)),
         ],
-    )(*tile_args)
-    from_ahead = lax.ppermute(ahead, "mesh", [(i + 1, i) for i in range(count - 1)])
-    from_behind = lax.ppermute(behind, "mesh", [(i, i + 1) for i in range(count - 1)])
+    )(tile_count, node_count, core, *tile_args[2:])
+    odd = range(1, count - 1, 2)
+    from_next = lax.ppermute(to_next, "mesh", [(i, i + 1) for i in odd] + [(i + 1, i) for i in odd])
+    from_chip = swap(to_chip)
     field, part = call(
         first_kernel, 2, 5, 0,
         [((nodes, width),), ((nodes, width),)],
@@ -522,11 +528,11 @@
         second_kernel, 3, 4, 5,
         [((nodes, 2 * BLK), BF16), ((nodes, 2 * BLK), BF16), ((BLK + 8, BLK),), ((BLK + 8, BLK),)],
         [
-            acc, pieces, pltpu.VMEM((nodes, BLK), BF16), pltpu.VMEM((nodes, BLK), BF16),
+            acc, pieces, pltpu.VMEM((nodes, 2 * BLK), BF16),
             chosen, index, index, lines, tiles, pltpu.SemaphoreType.DMA((4,)),
         ],
     )(tile_count, node_count, core, *map(stay, (tile_rows, tile_offsets, diag, tile_values)),
-      field, part, behind, from_behind, from_ahead)
+      field, part, behind, from_chip, from_next)
     total = keep + swap(give)
     total = total + functools.reduce(jnp.add, [moved(total, d, 0) for d in range(1, nx)])
     total = total + functools.reduce(jnp.add, [moved(total, 0, d) for d in range(1, ny)])

time: 122 us -> 113 us (0.926)
  starting transfers between devices: 30.3 us -> 26 us
  local copies, waits for them, and re-layouts: 4.43 us -> 0.68 us
    unnamed x14 -> x6, local copies, waits for them, and re-layouts: 3.76 us -> 0.02 us
    ppermute x6, starting transfers between devices: 11 us -> 8.52 us  [moved(): lax.ppermute(value, 'mesh', [(place(x, y, c), place(x + dx, y + dy, c)) f...]
    ppermute x3 -> x4, starting transfers between devices: 6.52 us -> 4.39 us  [swap(): return lax.ppermute(value, 'mesh', [(i, i ^ 1) for i in range(count)])]
    ppermute x2 -> x1, starting transfers between devices: 4.33 us -> 4.65 us  [body(): lax.ppermute(to_next, 'mesh', [(i, i + 1) for i in odd] + [(i + 1, i) for...]
    ppermute x3 -> x4, waiting for transfers between devices: 4.99 us -> 5 us  [swap(): return lax.ppermute(value, 'mesh', [(i, i ^ 1) for i in range(count)])]
  transfers between devices with their start and end apart: 12 -> 12, of which waited for: 9 -> 9; matrix products, arithmetic and copies ran while one was open for 0% -> 0% of each run, Pallas kernels for 6% -> 7%
where the time goes in v4:
time: 113 us
  blocking collectives  33.3 us (29%)
  Pallas kernels  27.3 us (24%)
  starting transfers between devices  26 us (23%)
  waiting for transfers between devices  20.5 us (18%)
  other arithmetic  2.74 us (2%)
  between operations  2.08 us (2%)
    all_to_all x1, blocking collectives, body(): lax.all_to_all(half, 'mesh', split_axis=0, concat_axis=0, tiled=True, axi...  33.3 us
    ppermute x6, starting transfers between devices, moved(): lax.ppermute(value, 'mesh', [(place(x, y, c), place(x + dx, y + dy, c)) f...  8.52 us
    all_to_all x1, starting transfers between devices, body(): lax.all_to_all(got.sum(0), 'elec', split_axis=0, concat_axis=1, tiled=True)  8.47 us
    pallas_call x1, Pallas kernels, body(): coef, = call(solve_kernel, 1, 0, 2, [((2 * BLK, BLK),)])(core, total, other)  8.44 us
    ppermute x6, waiting for transfers between devices, moved(): lax.ppermute(value, 'mesh', [(place(x, y, c), place(x + dx, y + dy, c)) f...  8.33 us
    all_to_all x1, waiting for transfers between devices, body(): lax.all_to_all(got.sum(0), 'elec', split_axis=0, concat_axis=1, tiled=True)  7.13 us
    pallas_call x1, Pallas kernels, body(): call(second_kernel, 3, 4, 5, [((nodes, 2 * BLK), BF16), ((nodes, 2 * BLK)...  5.69 us
    ppermute x4, waiting for transfers between devices, swap(): return lax.ppermute(value, 'mesh', [(i, i ^ 1) for i in range(count)])  5 us
  transfers between devices with their start and end apart: 12, of which 9 were waited for; matrix products, arithmetic and copies ran while one was open for 0% of the time, Pallas kernels for 7%

profile of v4, /device:TPU:8, one launch (start us, length us, event | category | flops | bytes accessed | tf_op | source)
XLA Modules:
  0.0 112.6 jit_solution(15105848882316460344)
XLA Ops:
  1.9 2.2 %shard_map.114 = (f32[256,128]{1,0:T(8,128)S(1)}, f32[520,128]{1,0:T(8,128)S(1)}, f32[520,128]{1,0:T(8,128)S(1)}) custom-call(s32[1]{0:T(128)S(6)} %copy.15.tcount, s32[1]{0:T(128)S(6)} %copy.16.ncount, s32[1]{0:T(128)} %bitcast.core, s32[64]{0:T(128)} %trow_far.5, s32[64]{0:T(128)} %toff_far.5, f32[2048,128]{1,0:T(8,128)} %rhs_far.3, f32[16,128]{1,0:T(8,128)} %bitcast.11, ...), custom_call_target="tpu_custom_call" | custom-call | tf_op jit(solution)/shard_map/pallas_call | solution.py:511
  4.1 0.2 collective-permute-start
  4.4 4.6 %collective-permute-start.1 = (f32[520,128]{1,0:T(8,128)S(1)}, f32[520,128]{1,0:T(8,128)S(1)}, u32[]{:S(2)}, u32[]{:S(2)}) collective-permute-start(f32[520,128]{1,0:T(8,128)S(1)} %get-tuple-element.19), channel_id=1, source_target_pairs={{8,16},{24,32},{40,48},{56,64},{72,80},{88,96},{104,112},{120,128}... | collective-permute-start | bytes 798728 | tf_op jit(solution)/shard_map/ppermute | solution.py:520
  9.0 4.6 %shard_map.113 = (f32[2048,128]{1,0:T(8,128)S(1)}, f32[2048,128]{1,0:T(8,128)S(1)}) custom-call(s32[1]{0:T(128)S(6)} %copy.15.tcount, s32[1]{0:T(128)S(6)} %copy.16.ncount, s32[64]{0:T(128)} %trow_far.5, s32[64]{0:T(128)} %toff_far.5, f32[2048,128]{1,0:T(8,128)} %rhs_far.3, f32[16,128]{1,0:T(8,128)} %bitcast.12, bf16[64,128,128]{2,1,0:T(8,128)(2,1)} %tiles_far.5), custom_call_target="tpu_custom_call" | custom-call | tf_op jit(solution)/shard_map/pallas_call | solution.py:522
  13.7 0.0 collective-permute-done.from_chip
  13.7 0.0 collective-permute-done.1.from_next
  13.7 0.0 copy-start
  13.7 0.0 copy-start.1
  13.7 5.7 %shard_map.115 = (bf16[2048,256]{1,0:T(8,128)(2,1)S(1)}, bf16[2048,256]{1,0:T(8,128)(2,1)S(1)}, f32[136,128]{1,0:T(8,128)S(1)}, f32[136,128]{1,0:T(8,128)S(1)}) custom-call(s32[1]{0:T(128)S(6)} %copy.15.tcount, s32[1]{0:T(128)S(6)} %copy.16.ncount, s32[1]{0:T(128)} %bitcast.core, s32[64]{0:T(128)} %trow_far.5, s32[64]{0:T(128)} %toff_far.5, ...), custom_call_target="tpu_custom_call" | custom-call | tf_op jit(solution)/shard_map/pallas_call | solution.py:527
  19.4 0.0 copy-start.2
  19.4 3.5 %collective-permute-start.2 = (f32[136,128]{1,0:T(8,128)S(1)}, f32[136,128]{1,0:T(8,128)S(1)}, u32[]{:S(2)}, u32[]{:S(2)}) collective-permute-start(f32[136,128]{1,0:T(8,128)S(1)} %get-tuple-element.23), channel_id=1, source_target_pairs={{0,8},{8,0},{16,24},{24,16},{32,40},{40,32},{48,56},{56,48},{64,72... | collective-permute-start | bytes 208904 | tf_op jit(solution)/shard_map/ppermute | solution.py:499
  22.9 0.9 collective-permute-done.2
  23.9 2.4 %collective-permute-start.5 = (f32[136,128]{1,0:T(8,128)S(1)}, f32[136,128]{1,0:T(8,128)S(1)}, u32[]{:S(2)}, u32[]{:S(2)}) collective-permute-start(f32[136,128]{1,0:T(8,128)S(1)} %add.29), channel_id=1, source_target_pairs={{0,192},{8,200},{16,208},{24,216},{32,224},{40,232},{48,240},{56,2... | collective-permute-start | bytes 208904 | tf_op jit(solution)/shard_map/ppermute | solution.py:493
  26.2 0.8 collective-permute-start.4
  27.1 1.3 %collective-permute-start.3 = (f32[136,128]{1,0:T(8,128)S(1)}, f32[136,128]{1,0:T(8,128)S(1)}, u32[]{:S(2)}, u32[]{:S(2)}) collective-permute-start(f32[136,128]{1,0:T(8,128)S(1)} %add.29), channel_id=1, source_target_pairs={{0,64},{8,72},{16,80},{24,88},{32,96},{40,104},{48,112},{56,120},{... | collective-permute-start | bytes 208904 | tf_op jit(solution)/shard_map/ppermute | solution.py:493
  28.4 0.0 collective-permute-done.5
  28.4 4.3 %collective-permute-done.4 = f32[136,128]{1,0:T(8,128)S(1)} collective-permute-done((f32[136,128]{1,0:T(8,128)S(1)}, f32[136,128]{1,0:T(8,128)S(1)}, u32[]{:S(2)}, u32[]{:S(2)}) %collective-permute-start.4) | collective-permute-done | bytes 69664 | tf_op jit(solution)/shard_map/ppermute | solution.py:493
  32.7 0.7 collective-permute-done.3
  33.4 0.9 collective-permute-start.8
  34.3 2.1 %collective-permute-start.7 = (f32[136,128]{1,0:T(8,128)S(1)}, f32[136,128]{1,0:T(8,128)S(1)}, u32[]{:S(2)}, u32[]{:S(2)}) collective-permute-start(f32[136,128]{1,0:T(8,128)S(1)} %add_add_fusion.1), channel_id=1, source_target_pairs={{0,32},{8,40},{16,48},{24,56},{32,0},{40,8},{48,16},{56,24},{64,96... | collective-permute-start | bytes 208904 | tf_op jit(solution)/shard_map/ppermute | solution.py:493
  36.4 1.0 collective-permute-start.6
  37.4 0.4 collective-permute-done.8
  37.8 2.3 %collective-permute-done.7 = f32[136,128]{1,0:T(8,128)S(1)} collective-permute-done((f32[136,128]{1,0:T(8,128)S(1)}, f32[136,128]{1,0:T(8,128)S(1)}, u32[]{:S(2)}, u32[]{:S(2)}) %collective-permute-start.7) | collective-permute-done | bytes 69664 | tf_op jit(solution)/shard_map/ppermute | solution.py:493
  40.1 0.6 collective-permute-done.6
  40.8 0.3 collective-permute-start.9
  41.0 0.0 copy-done
  41.0 0.0 copy-done.1
  41.1 1.0 shard_map.118
  42.1 0.2 collective-permute-done.9.other
  42.3 8.4 %shard_map.116.coef = f32[256,128]{1,0:T(8,128)S(1)} custom-call(s32[1]{0:T(128)} %bitcast.core, f32[136,128]{1,0:T(8,128)S(1)} %add_add_fusion.mine, f32[136,128]{1,0:T(8,128)S(1)} %collective-permute-done.9.other), custom_call_target="tpu_custom_call" | custom-call | tf_op jit(solution)/shard_map/pallas_call | solution.py:544
  50.7 0.0 copy-done.2
  50.7 3.3 %shard_map.119 = (f32[32,128,128]{2,1,0:T(8,128)S(1)}, f32[32,128,128]{2,1,0:T(8,128)S(1)}) custom-call(s32[16]{0:T(128)S(1)} %copy-done.2, s32[1]{0:T(128)} %bitcast.core, bf16[2048,256]{1,0:T(8,128)(2,1)S(1)} %get-tuple-element.24.left_h, bf16[2048,256]{1,0:T(8,128)(2,1)S(1)} %get-tuple-element.25.left_l, f32[256,128]{1,0:T(8,128)S(1)} %shard_map.116.coef), custom_call_target="tpu_custom_call" | custom-call | tf_op jit(solution)/shard_map/pallas_call | solution.py:545
  54.1 0.4 collective-permute-start.10
  54.5 3.9 %collective-permute-done.10 = f32[32,128,128]{2,1,0:T(8,128)S(1)} collective-permute-done((f32[32,128,128]{2,1,0:T(8,128)S(1)}, f32[32,128,128]{2,1,0:T(8,128)S(1)}, u32[]{:S(2)}, u32[]{:S(2)}) %collective-permute-start.10) | collective-permute-done | bytes 2097184 | tf_op jit(solution)/shard_map/ppermute | solution.py:499
  58.3 0.3 add.36
  58.7 33.3 %all_to_all.24 = f32[16,256,128]{2,1,0:T(8,128)} all-to-all(f32[16,256,128]{2,1,0:T(8,128)S(1)} %bitcast.10), channel_id=1, replica_groups={{0,16,32,48,64,80,96,112,128,144,160,176,192,208,224,240},{8,24,40,56,7..., dimensions={0} | all-to-all | bytes 4194304 | tf_op jit(solution)/shard_map/all_to_all | solution.py:552
  92.0 2.4 %reduce_sum.9 = f32[256,128]{1,0:T(8,128)} reduce(f32[16,256,128]{2,1,0:T(8,128)} %all_to_all.24, f32[]{:T(128)} %constant.20.clone.1), dimensions={0}, to_apply=%region_0.1 | reduce | flops 491520 | bytes 2228228 | tf_op jit(solution)/shard_map/reduce_sum | solution.py:555
  94.4 8.5 %all-to-all-start.1 = ((f32[8,32,128]{2,1,0:T(8,128)}), f32[8,32,128]{2,1,0:T(8,128)S(1)}, u32[]{:S(2)}, u32[]{:S(2)}) async-start(f32[8,32,128]{2,1,0:T(8,128)} %bitcast.3), calls=%async_computation.1 | async-start | bytes 262144 | tf_op jit(solution)/shard_map/all_to_all | solution.py:555
  102.8 1.9 %shard_map.117 = f32[2048,128]{1,0:T(8,128)} custom-call(bf16[2048,256]{1,0:T(8,128)(2,1)S(1)} %get-tuple-element.20.left_h.wide_h, bf16[2048,256]{1,0:T(8,128)(2,1)S(1)} %get-tuple-element.21.left_l.wide_l, f32[256,128]{1,0:T(8,128)S(1)} %shard_map.116.coef), custom_call_target="tpu_custom_call" | custom-call | tf_op jit(solution)/shard_map/pallas_call | solution.py:549
  104.8 7.1 %all-to-all-done.1 = f32[8,32,128]{2,1,0:T(8,128)S(1)} async-done(((f32[8,32,128]{2,1,0:T(8,128)}), f32[8,32,128]{2,1,0:T(8,128)S(1)}, u32[]{:S(2)}, u32[]{:S(2)}) %all-to-all-start.1) | async-done | bytes 131104 | tf_op jit(solution)/shard_map/all_to_all | solution.py:555
  111.9 0.7 copy_bitcast_fusion
  (3 shorter events, 0.1 us)
Async XLA Ops:
  4.1 9.5 %collective-permute-start = (f32[520,128]{1,0:T(8,128)S(1)}, f32[520,128]{1,0:T(8,128)S(1)}, u32[]{:S(2)}, u32[]{:S(2)}) collective-permute-start(f32[520,128]{1,0:T(8,128)S(1)} %get-tuple-element.18), channel_id=1, source_target_pairs={{0,8},{8,0},{16,24},{24,16},{32,40},{40,32},{48,56},{56,48},{64,72... | collective-permute-start | bytes 798728 | tf_op jit(solution)/shard_map/ppermute | solution.py:499
  4.4 9.3 %collective-permute-start.1 = (f32[520,128]{1,0:T(8,128)S(1)}, f32[520,128]{1,0:T(8,128)S(1)}, u32[]{:S(2)}, u32[]{:S(2)}) collective-permute-start(f32[520,128]{1,0:T(8,128)S(1)} %get-tuple-element.19), channel_id=1, source_target_pairs={{8,16},{24,32},{40,48},{56,64},{72,80},{88,96},{104,112},{120,128}... | collective-permute-start | bytes 798728 | tf_op jit(solution)/shard_map/ppermute | solution.py:520
  13.7 27.4 %copy-start = (bf16[16,128,128]{2,1,0:T(8,128)(2,1)S(1)}, bf16[16,128,128]{2,1,0:T(8,128)(2,1)}, u32[]{:S(2)}) copy-start(bf16[16,128,128]{2,1,0:T(8,128)(2,1)} %inc.1) | copy-start | bytes 1572868
  13.7 27.4 %copy-start.1 = (s32[16]{0:T(128)S(1)}, s32[16]{0:T(128)}, u32[]{:S(2)}) copy-start(s32[16]{0:T(128)} %irow.1) | copy-start | bytes 196
  19.4 31.3 %copy-start.2 = (s32[16]{0:T(128)S(1)}, s32[16]{0:T(128)}, u32[]{:S(2)}) copy-start(s32[16]{0:T(128)} %iblk.1) | copy-start | bytes 196
  19.4 4.4 %collective-permute-start.2 = (f32[136,128]{1,0:T(8,128)S(1)}, f32[136,128]{1,0:T(8,128)S(1)}, u32[]{:S(2)}, u32[]{:S(2)}) collective-permute-start(f32[136,128]{1,0:T(8,128)S(1)} %get-tuple-element.23), channel_id=1, source_target_pairs={{0,8},{8,0},{16,24},{24,16},{32,40},{40,32},{48,56},{56,48},{64,72... | collective-permute-start | bytes 208904 | tf_op jit(solution)/shard_map/ppermute | solution.py:499
  23.9 4.5 %collective-permute-start.5 = (f32[136,128]{1,0:T(8,128)S(1)}, f32[136,128]{1,0:T(8,128)S(1)}, u32[]{:S(2)}, u32[]{:S(2)}) collective-permute-start(f32[136,128]{1,0:T(8,128)S(1)} %add.29), channel_id=1, source_target_pairs={{0,192},{8,200},{16,208},{24,216},{32,224},{40,232},{48,240},{56,2... | collective-permute-start | bytes 208904 | tf_op jit(solution)/shard_map/ppermute | solution.py:493
  26.2 6.4 %collective-permute-start.4 = (f32[136,128]{1,0:T(8,128)S(1)}, f32[136,128]{1,0:T(8,128)S(1)}, u32[]{:S(2)}, u32[]{:S(2)}) collective-permute-start(f32[136,128]{1,0:T(8,128)S(1)} %add.29), channel_id=1, source_target_pairs={{0,128},{8,136},{16,144},{24,152},{32,160},{40,168},{48,176},{56,1... | collective-permute-start | bytes 208904 | tf_op jit(solution)/shard_map/ppermute | solution.py:493
  27.1 6.3 %collective-permute-start.3 = (f32[136,128]{1,0:T(8,128)S(1)}, f32[136,128]{1,0:T(8,128)S(1)}, u32[]{:S(2)}, u32[]{:S(2)}) collective-permute-start(f32[136,128]{1,0:T(8,128)S(1)} %add.29), channel_id=1, source_target_pairs={{0,64},{8,72},{16,80},{24,88},{32,96},{40,104},{48,112},{56,120},{... | collective-permute-start | bytes 208904 | tf_op jit(solution)/shard_map/ppermute | solution.py:493
  33.4 4.4 %collective-permute-start.8 = (f32[136,128]{1,0:T(8,128)S(1)}, f32[136,128]{1,0:T(8,128)S(1)}, u32[]{:S(2)}, u32[]{:S(2)}) collective-permute-start(f32[136,128]{1,0:T(8,128)S(1)} %add_add_fusion.1), channel_id=1, source_target_pairs={{0,48},{8,56},{16,0},{24,8},{32,16},{40,24},{48,32},{56,40},{64,11... | collective-permute-start | bytes 208904 | tf_op jit(solution)/shard_map/ppermute | solution.py:493
  34.3 5.8 %collective-permute-start.7 = (f32[136,128]{1,0:T(8,128)S(1)}, f32[136,128]{1,0:T(8,128)S(1)}, u32[]{:S(2)}, u32[]{:S(2)}) collective-permute-start(f32[136,128]{1,0:T(8,128)S(1)} %add_add_fusion.1), channel_id=1, source_target_pairs={{0,32},{8,40},{16,48},{24,56},{32,0},{40,8},{48,16},{56,24},{64,96... | collective-permute-start | bytes 208904 | tf_op jit(solution)/shard_map/ppermute | solution.py:493
  36.4 4.3 %collective-permute-start.6 = (f32[136,128]{1,0:T(8,128)S(1)}, f32[136,128]{1,0:T(8,128)S(1)}, u32[]{:S(2)}, u32[]{:S(2)}) collective-permute-start(f32[136,128]{1,0:T(8,128)S(1)} %add_add_fusion.1), channel_id=1, source_target_pairs={{0,16},{8,24},{16,32},{24,40},{32,48},{40,56},{48,0},{56,8},{64,80... | collective-permute-start | bytes 208904 | tf_op jit(solution)/shard_map/ppermute | solution.py:493
  40.8 1.5 %collective-permute-start.9 = (f32[136,128]{1,0:T(8,128)S(1)}, f32[136,128]{1,0:T(8,128)S(1)}, u32[]{:S(2)}, u32[]{:S(2)}) collective-permute-start(f32[136,128]{1,0:T(8,128)S(1)} %add_add_fusion.mine), channel_id=1, source_target_pairs={{0,8},{8,0},{16,24},{24,16},{32,40},{40,32},{48,56},{56,48},{64,72... | collective-permute-start | bytes 208904 | tf_op jit(solution)/shard_map/ppermute | solution.py:499
  54.1 4.2 %collective-permute-start.10 = (f32[32,128,128]{2,1,0:T(8,128)S(1)}, f32[32,128,128]{2,1,0:T(8,128)S(1)}, u32[]{:S(2)}, u32[]{:S(2)}) collective-permute-start(f32[32,128,128]{2,1,0:T(8,128)S(1)} %get-tuple-element.27), channel_id=1, source_target_pairs={{0,8},{8,0},{16,24},{24,16},{32,40},{40,32},{48,56},{56,48},{64,72... | collective-permute-start | bytes 6291464 | tf_op jit(solution)/shard_map/ppermute | solution.py:499
  94.4 17.6 %all-to-all-start.1 = ((f32[8,32,128]{2,1,0:T(8,128)}), f32[8,32,128]{2,1,0:T(8,128)S(1)}, u32[]{:S(2)}, u32[]{:S(2)}) async-start(f32[8,32,128]{2,1,0:T(8,128)} %bitcast.3), calls=%async_computation.1 | async-start | bytes 262144 | tf_op jit(solution)/shard_map/all_to_all | solution.py:555

commit v5 on v4

--- a/solution.py
+++ b/solution.py
@@ -14,18 +14,12 @@
 SHIFT = 2.0
 F32 = jnp.float32
 BF16 = jnp.bfloat16
-HIGHEST = lax.Precision.HIGHEST
-GROUP = 4
+GROUP = 8
+TILE_GROUP = 16
 
 
 def mm(left, right, dims=((1,), (0,))):
     return lax.dot_general(left, right, (dims, ((), ())), preferred_element_type=F32)
-
-
-def mmh(left, right, dims=((1,), (0,))):
-    return lax.dot_general(
-        left, right, (dims, ((), ())), preferred_element_type=F32, precision=HIGHEST
-    )
 
 
 def split(value):
@@ -41,14 +35,14 @@
     return jnp.transpose(jnp.broadcast_to(line, (BLK, BLK)))
 
 
-def grouped(count, one):
+def grouped(count, one, size=GROUP):
     def group(g, carry):
-        for add in [one(g * GROUP + k, g * GROUP + k < count) for k in range(GROUP)]:
+        for add in [one(g * size + k, g * size + k < count) for k in range(size)]:
             for target, index, value in add:
                 target[index] += value
         return carry
 
-    lax.fori_loop(0, (count + GROUP - 1) // GROUP, group, 0)
+    lax.fori_loop(0, (count + size - 1) // size, group, 0)
 
 
 def chosen_loop(count, trow, toff, chosen, wanted, one):
@@ -201,7 +195,7 @@
             (acc, jnp.where(inside, c, spare), backward(tile, pieces[r])),
         )
 
-    grouped(tcount[0], one)
+    grouped(tcount[0], one, TILE_GROUP)
 
     def finish(b):
         part[block_at(b), :] = jnp.where(rows_of(b) < live, acc[b], 0.0)
@@ -288,7 +282,7 @@
         value = forward(tiles[t], pieces[r + toff[t]])
         return ((acc, jnp.where(on, r, spare), value),)
 
-    grouped(count, one)
+    grouped(count, one, TILE_GROUP)
 
     def widen(b):
         high, low = split(acc[b])
@@ -345,6 +339,14 @@
     rest = value - high
     middle = rest.astype(BF16).astype(F32)
     return high, middle, rest - middle
+
+
+def square(left, right):
+    lh, lm, ll = (part.astype(BF16) for part in thirds(left))
+    rh, rm, rl = (part.astype(BF16) for part in thirds(right))
+    small = mm(jnp.concatenate([lm, ll], 1), jnp.concatenate([rm, rh], 0))
+    middle = mm(jnp.concatenate([lh, lm], 1), jnp.concatenate([rm, rh], 0))
+    return mm(jnp.concatenate([lh, lh], 1), jnp.concatenate([rh, rl], 0)) + (middle + small)
 
 
 def stacked(left, right):
@@ -405,11 +407,11 @@
     m2 = n2 + SHIFT * n1
     m3 = n3 + SHIFT * n2
     inverse = invert(m1)
-    both = mmh(inverse, jnp.concatenate([m2, n0], 1))
-    across = mmh(m2, both)
+    both = square(inverse, jnp.concatenate([m2, n0], 1))
+    across = square(m2, both)
     schur = m3 - across[:, :BLK]
-    y1 = mmh(invert(schur), n1 - across[:, BLK:])
-    y0 = both[:, BLK:] - mmh(both[:, :BLK], y1)
+    y1 = square(invert(schur), n1 - across[:, BLK:])
+    y0 = both[:, BLK:] - square(both[:, :BLK], y1)
     out[:BLK, :] = y0
     out[BLK:, :] = y1
 
@@ -428,35 +430,34 @@
     return mm(left_h, high) + (mm(left_h, low) + mm(left_l, high))
 
 
-def scatter_kernel(iblk, core, left_h, left_l, coef, keep, give):
-    keep[...] = jnp.zeros(keep.shape, F32)
-    give[...] = jnp.zeros(give.shape, F32)
+def scatter(iblk, wanted, out, value_at):
+    out[...] = jnp.zeros(out.shape, F32)
+    for u in range(iblk.shape[0]):
+        block = iblk[u]
+        owner = block // SRCB_DEV
+        to = owner // 2 * SRCB_DEV + block % SRCB_DEV
+
+        @pl.when(owner % 2 == wanted)
+        def _():
+            out[to] += value_at(u)
+
+
+def scatter_kernel(iblk, core, left_h, left_l, coef, give, products):
     weights = coef[...]
-    for g in range(left_h.shape[0] // (GROUP * BLK)):
-        at = slice(g * GROUP * BLK, (g + 1) * GROUP * BLK)
-        product = combine(left_h[at, :], left_l[at, :], weights)
-        for k in range(GROUP):
-            value = product[k * BLK : (k + 1) * BLK, :]
-            block = iblk[g * GROUP + k]
-            owner = block // SRCB_DEV
-            to = owner // 2 * SRCB_DEV + block % SRCB_DEV
-            mine = owner % 2 == core[0]
-
-            @pl.when(mine)
-            def _():
-                keep[to] += value
-
-            @pl.when(jnp.logical_not(mine))
-            def _():
-                give[to] += value
-
-
-def third_kernel(left_h, left_l, coef, sol):
+    step = GROUP * BLK
+    for g in range(products.shape[0] // step):
+        at = slice(g * step, (g + 1) * step)
+        products[at, :] = combine(left_h[at, :], left_l[at, :], weights)
+    scatter(iblk, 1 - core[0], give, lambda u: products[u * BLK : (u + 1) * BLK, :])
+
+
+def third_kernel(iblk, core, left_h, left_l, coef, products, sol, keep):
     weights = coef[...]
     step = GROUP * BLK
     for g in range(sol.shape[0] // step):
         at = slice(g * step, (g + 1) * step)
         sol[at, :] = combine(left_h[at, :], left_l[at, :], weights)
+    scatter(iblk, core[0], keep, lambda u: products[u * BLK : (u + 1) * BLK, :])
 
 
 def call(kernel, n_scalar, n_far, n_vector, outs, scratch=(), mib=16):
@@ -542,11 +543,13 @@
         gather_kernel, 1, 0, 3, [((rows, 2 * BLK), BF16), ((rows, 2 * BLK), BF16)]
     )(inc_rows, wide_h, wide_l, inc_values)
     (coef,) = call(solve_kernel, 1, 0, 2, [((2 * BLK, BLK),)])(core, total, other)
-    keep, give = call(scatter_kernel, 2, 0, 3, [((lead_half, BLK, BLK),)] * 2)(
-        inc_blocks, core, gather_h, gather_l, coef
-    )
+    give, products = call(
+        scatter_kernel, 2, 0, 3, [((lead_half, BLK, BLK),), ((rows, BLK),)]
+    )(inc_blocks, core, gather_h, gather_l, coef)
     other = swap(give)
-    (solution,) = call(third_kernel, 0, 0, 3, [((nodes, width),)])(wide_h, wide_l, coef)
+    solution, keep = call(
+        third_kernel, 2, 0, 4, [((nodes, width),), ((lead_half, BLK, BLK),)]
+    )(inc_blocks, core, wide_h, wide_l, coef, products)
     half = (keep + other).reshape(nx * ny, SRCB_DEV * BLK, width)
     groups = [[2 * i + c for i in range(nx * ny)] for c in range(2)]
     got = lax.all_to_all(

time: 113 us -> 106 us (0.938)
  blocking collectives: 33.3 us -> 50.7 us
  starting transfers between devices: 26 us -> 16 us
  waiting for transfers between devices: 20.5 us -> 10.8 us
  Pallas kernels: 27.3 us -> 24.6 us
  other arithmetic: 2.74 us -> 0.49 us
    all_to_all x0 -> x1, blocking collectives: none -> 17.3 us  [body(): lax.all_to_all(got.sum(0), 'elec', split_axis=0, concat_axis=1, tiled=True)]
    all_to_all x1 -> x0, starting transfers between devices: 8.47 us -> none  [body(): lax.all_to_all(got.sum(0), 'elec', split_axis=0, concat_axis=1, tiled=True)]
    all_to_all x1 -> x0, waiting for transfers between devices: 7.13 us -> none  [body(): lax.all_to_all(got.sum(0), 'elec', split_axis=0, concat_axis=1, tiled=True)]
    ppermute x4, waiting for transfers between devices: 5 us -> 2.08 us  [swap(): return lax.ppermute(value, 'mesh', [(i, i ^ 1) for i in range(count)])]
    ppermute x4, starting transfers between devices: 4.39 us -> 1.7 us  [swap(): return lax.ppermute(value, 'mesh', [(i, i ^ 1) for i in range(count)])]
    reduce_sum x1, other arithmetic: 2.35 us -> 0.1 us  [body(): got.sum(0)]
    ppermute x6, starting transfers between devices: 8.52 us -> 9.68 us  [moved(): lax.ppermute(value, 'mesh', [(place(x, y, c), place(x + dx, y + dy, c)) f...]
  transfers between devices with their start and end apart: 12 -> 11, of which waited for: 9 -> 8; matrix products, arithmetic and copies ran while one was open for 0% -> 0% of each run, Pallas kernels for 7% -> 7%
where the time goes in v5:
time: 106 us; the launch traced here: 105 us
  blocking collectives  50.7 us (48%)
  Pallas kernels  24.6 us (23%)
  starting transfers between devices  16 us (15%)
  waiting for transfers between devices  10.8 us (10%)
  between operations  2.07 us (2%)
    all_to_all x1, blocking collectives, body(): lax.all_to_all(half, 'mesh', split_axis=0, concat_axis=0, tiled=True, axi...  33.3 us
    all_to_all x1, blocking collectives, body(): lax.all_to_all(got.sum(0), 'elec', split_axis=0, concat_axis=1, tiled=True)  17.3 us
    ppermute x6, starting transfers between devices, moved(): lax.ppermute(value, 'mesh', [(place(x, y, c), place(x + dx, y + dy, c)) f...  9.68 us
    pallas_call x1, Pallas kernels, body(): coef, = call(solve_kernel, 1, 0, 2, [((2 * BLK, BLK),)])(core, total, other)  8.23 us
    ppermute x6, waiting for transfers between devices, moved(): lax.ppermute(value, 'mesh', [(place(x, y, c), place(x + dx, y + dy, c)) f...  8.18 us
    pallas_call x1, Pallas kernels, body(): call(second_kernel, 3, 4, 5, [((nodes, 2 * BLK), BF16), ((nodes, 2 * BLK)...  4.7 us
    ppermute x1, starting transfers between devices, body(): lax.ppermute(to_next, 'mesh', [(i, i + 1) for i in odd] + [(i + 1, i) for...  4.61 us
    pallas_call x1, Pallas kernels, body(): call(first_kernel, 2, 5, 0, [((nodes, width),), ((nodes, width),)], [acc,...  3.56 us
  transfers between devices with their start and end apart: 11, of which 8 were waited for; matrix products, arithmetic and copies ran while one was open for 0% of the time, Pallas kernels for 7%

profile of v5, /device:TPU:8, one launch (start us, length us, event | category | flops | bytes accessed | tf_op | source)
XLA Modules:
  0.0 105.3 jit_solution(7712843202992744352)
XLA Ops:
  1.9 2.4 %shard_map.114 = (f32[256,128]{1,0:T(8,128)S(1)}, f32[520,128]{1,0:T(8,128)S(1)}, f32[520,128]{1,0:T(8,128)S(1)}) custom-call(s32[1]{0:T(128)S(6)} %copy.15.tcount, s32[1]{0:T(128)S(6)} %copy.16.ncount, s32[1]{0:T(128)} %bitcast.core, s32[64]{0:T(128)} %trow_far.5, s32[64]{0:T(128)} %toff_far.5, f32[2048,128]{1,0:T(8,128)} %rhs_far.3, f32[16,128]{1,0:T(8,128)} %bitcast.12, ...), custom_call_target="tpu_custom_call" | custom-call | tf_op jit(solution)/shard_map/pallas_call | solution.py:512
  4.3 0.1 collective-permute-start
  4.4 4.6 %collective-permute-start.1 = (f32[520,128]{1,0:T(8,128)S(1)}, f32[520,128]{1,0:T(8,128)S(1)}, u32[]{:S(2)}, u32[]{:S(2)}) collective-permute-start(f32[520,128]{1,0:T(8,128)S(1)} %get-tuple-element.21), channel_id=1, source_target_pairs={{8,16},{24,32},{40,48},{56,64},{72,80},{88,96},{104,112},{120,128}... | collective-permute-start | bytes 798728 | tf_op jit(solution)/shard_map/ppermute | solution.py:521
  9.0 3.6 %shard_map.113 = (f32[2048,128]{1,0:T(8,128)S(1)}, f32[2048,128]{1,0:T(8,128)S(1)}) custom-call(s32[1]{0:T(128)S(6)} %copy.15.tcount, s32[1]{0:T(128)S(6)} %copy.16.ncount, s32[64]{0:T(128)} %trow_far.5, s32[64]{0:T(128)} %toff_far.5, f32[2048,128]{1,0:T(8,128)} %rhs_far.3, f32[16,128]{1,0:T(8,128)} %bitcast.13, bf16[64,128,128]{2,1,0:T(8,128)(2,1)} %tiles_far.5), custom_call_target="tpu_custom_call" | custom-call | tf_op jit(solution)/shard_map/pallas_call | solution.py:523
  12.6 0.0 collective-permute-done.from_chip
  12.6 0.5 collective-permute-done.1.from_next
  13.1 0.0 copy-start
  13.1 0.0 copy-start.2
  13.1 4.7 %shard_map.115 = (bf16[2048,256]{1,0:T(8,128)(2,1)S(1)}, bf16[2048,256]{1,0:T(8,128)(2,1)S(1)}, f32[136,128]{1,0:T(8,128)S(1)}, f32[136,128]{1,0:T(8,128)S(1)}) custom-call(s32[1]{0:T(128)S(6)} %copy.15.tcount, s32[1]{0:T(128)S(6)} %copy.16.ncount, s32[1]{0:T(128)} %bitcast.core, s32[64]{0:T(128)} %trow_far.5, s32[64]{0:T(128)} %toff_far.5, ...), custom_call_target="tpu_custom_call" | custom-call | tf_op jit(solution)/shard_map/pallas_call | solution.py:528
  17.8 0.0 copy-start.1
  17.8 0.9 collective-permute-start.2
  18.8 0.9 collective-permute-done.2
  19.7 3.3 %collective-permute-start.5 = (f32[136,128]{1,0:T(8,128)S(1)}, f32[136,128]{1,0:T(8,128)S(1)}, u32[]{:S(2)}, u32[]{:S(2)}) collective-permute-start(f32[136,128]{1,0:T(8,128)S(1)} %add.29), channel_id=1, source_target_pairs={{0,192},{8,200},{16,208},{24,216},{32,224},{40,232},{48,240},{56,2... | collective-permute-start | bytes 208904 | tf_op jit(solution)/shard_map/ppermute | solution.py:494
  23.0 0.3 collective-permute-start.4
  23.3 0.9 collective-permute-start.3
  24.2 2.2 %collective-permute-done.5 = f32[136,128]{1,0:T(8,128)S(1)} collective-permute-done((f32[136,128]{1,0:T(8,128)S(1)}, f32[136,128]{1,0:T(8,128)S(1)}, u32[]{:S(2)}, u32[]{:S(2)}) %collective-permute-start.5) | collective-permute-done | bytes 69664 | tf_op jit(solution)/shard_map/ppermute | solution.py:494
  26.5 2.9 %collective-permute-done.4 = f32[136,128]{1,0:T(8,128)S(1)} collective-permute-done((f32[136,128]{1,0:T(8,128)S(1)}, f32[136,128]{1,0:T(8,128)S(1)}, u32[]{:S(2)}, u32[]{:S(2)}) %collective-permute-start.4) | collective-permute-done | bytes 69664 | tf_op jit(solution)/shard_map/ppermute | solution.py:494
  29.4 0.5 collective-permute-done.3
  29.9 1.8 %collective-permute-start.8 = (f32[136,128]{1,0:T(8,128)S(1)}, f32[136,128]{1,0:T(8,128)S(1)}, u32[]{:S(2)}, u32[]{:S(2)}) collective-permute-start(f32[136,128]{1,0:T(8,128)S(1)} %add_add_fusion.1), channel_id=1, source_target_pairs={{0,48},{8,56},{16,0},{24,8},{32,16},{40,24},{48,32},{56,40},{64,11... | collective-permute-start | bytes 208904 | tf_op jit(solution)/shard_map/ppermute | solution.py:494
  31.8 0.8 collective-permute-start.7
  32.6 2.5 %collective-permute-start.6 = (f32[136,128]{1,0:T(8,128)S(1)}, f32[136,128]{1,0:T(8,128)S(1)}, u32[]{:S(2)}, u32[]{:S(2)}) collective-permute-start(f32[136,128]{1,0:T(8,128)S(1)} %add_add_fusion.1), channel_id=1, source_target_pairs={{0,16},{8,24},{16,32},{24,40},{32,48},{40,56},{48,0},{56,8},{64,80... | collective-permute-start | bytes 208904 | tf_op jit(solution)/shard_map/ppermute | solution.py:494
  35.1 0.0 collective-permute-done.8
  35.1 2.5 %collective-permute-done.7 = f32[136,128]{1,0:T(8,128)S(1)} collective-permute-done((f32[136,128]{1,0:T(8,128)S(1)}, f32[136,128]{1,0:T(8,128)S(1)}, u32[]{:S(2)}, u32[]{:S(2)}) %collective-permute-start.7) | collective-permute-done | bytes 69664 | tf_op jit(solution)/shard_map/ppermute | solution.py:494
  37.6 0.0 collective-permute-done.6
  37.6 0.3 collective-permute-start.9
  37.9 0.0 copy-done
  37.9 0.0 copy-done.2
  37.9 1.0 shard_map.117
  38.9 0.2 collective-permute-done.9.other
  39.1 8.2 %shard_map.116.coef = f32[256,128]{1,0:T(8,128)S(1)} custom-call(s32[1]{0:T(128)} %bitcast.core, f32[136,128]{1,0:T(8,128)S(1)} %add_add_fusion.mine, f32[136,128]{1,0:T(8,128)S(1)} %collective-permute-done.9.other), custom_call_target="tpu_custom_call" | custom-call | tf_op jit(solution)/shard_map/pallas_call | solution.py:545
  47.4 0.0 copy-done.1
  47.4 1.9 %shard_map.118 = (f32[32,128,128]{2,1,0:T(8,128)S(1)}, f32[2048,128]{1,0:T(8,128)S(1)}) custom-call(s32[16]{0:T(128)S(1)} %copy-done.1, s32[1]{0:T(128)} %bitcast.core, bf16[2048,256]{1,0:T(8,128)(2,1)S(1)} %get-tuple-element.26.left_h, bf16[2048,256]{1,0:T(8,128)(2,1)S(1)} %get-tuple-element.27.left_l, f32[256,128]{1,0:T(8,128)S(1)} %shard_map.116.coef), custom_call_target="tpu_custom_call" | custom-call | tf_op jit(solution)/shard_map/pallas_call | solution.py:546
  49.3 0.4 collective-permute-start.10
  49.7 2.9 %shard_map.119 = (f32[2048,128]{1,0:T(8,128)}, f32[32,128,128]{2,1,0:T(8,128)S(1)}) custom-call(s32[16]{0:T(128)S(1)} %copy-done.1, s32[1]{0:T(128)} %bitcast.core, bf16[2048,256]{1,0:T(8,128)(2,1)S(1)} %get-tuple-element.22.wide_h.left_h, bf16[2048,256]{1,0:T(8,128)(2,1)S(1)} %get-tuple-element.23.wide_l.left_l, f32[256,128]{1,0:T(8,128)S(1)} %shard_map.116.coef, ...), custom_call_target="tpu_custom_call" | custom-call | tf_op jit(solution)/shard_map/pallas_call | solution.py:550
  52.6 1.0 collective-permute-done.10
  53.5 0.3 add.36
  53.9 33.3 %all_to_all.24 = f32[16,256,128]{2,1,0:T(8,128)S(1)} all-to-all(f32[16,256,128]{2,1,0:T(8,128)S(1)} %bitcast.10), channel_id=1, replica_groups={{0,16,32,48,64,80,96,112,128,144,160,176,192,208,224,240},{8,24,40,56,7..., dimensions={0} | all-to-all | bytes 4194304 | tf_op jit(solution)/shard_map/all_to_all | solution.py:555
  87.2 0.1 reduce_sum.9
  87.3 17.3 %all_to_all.25 = f32[8,32,128]{2,1,0:T(8,128)S(1)} all-to-all(f32[8,32,128]{2,1,0:T(8,128)S(1)} %bitcast.11), channel_id=1, replica_groups=mesh['mesh'=32,'elec'=8] {'elec'}, dimensions={0} | all-to-all | bytes 262144 | tf_op jit(solution)/shard_map/all_to_all | solution.py:558
  104.7 0.7 copy_bitcast_fusion
  (3 shorter events, 0.1 us)
Async XLA Ops:
  4.3 8.3 %collective-permute-start = (f32[520,128]{1,0:T(8,128)S(1)}, f32[520,128]{1,0:T(8,128)S(1)}, u32[]{:S(2)}, u32[]{:S(2)}) collective-permute-start(f32[520,128]{1,0:T(8,128)S(1)} %get-tuple-element.20), channel_id=1, source_target_pairs={{0,8},{8,0},{16,24},{24,16},{32,40},{40,32},{48,56},{56,48},{64,72... | collective-permute-start | bytes 798728 | tf_op jit(solution)/shard_map/ppermute | solution.py:500
  4.4 8.7 %collective-permute-start.1 = (f32[520,128]{1,0:T(8,128)S(1)}, f32[520,128]{1,0:T(8,128)S(1)}, u32[]{:S(2)}, u32[]{:S(2)}) collective-permute-start(f32[520,128]{1,0:T(8,128)S(1)} %get-tuple-element.21), channel_id=1, source_target_pairs={{8,16},{24,32},{40,48},{56,64},{72,80},{88,96},{104,112},{120,128}... | collective-permute-start | bytes 798728 | tf_op jit(solution)/shard_map/ppermute | solution.py:521
  13.1 24.8 %copy-start = (bf16[16,128,128]{2,1,0:T(8,128)(2,1)S(1)}, bf16[16,128,128]{2,1,0:T(8,128)(2,1)}, u32[]{:S(2)}) copy-start(bf16[16,128,128]{2,1,0:T(8,128)(2,1)} %inc.1) | copy-start | bytes 1572868
  13.1 24.8 %copy-start.2 = (s32[16]{0:T(128)S(1)}, s32[16]{0:T(128)}, u32[]{:S(2)}) copy-start(s32[16]{0:T(128)} %irow.1) | copy-start | bytes 196
  17.8 29.6 %copy-start.1 = (s32[16]{0:T(128)S(1)}, s32[16]{0:T(128)}, u32[]{:S(2)}) copy-start(s32[16]{0:T(128)} %iblk.3) | copy-start | bytes 196
  17.8 1.9 %collective-permute-start.2 = (f32[136,128]{1,0:T(8,128)S(1)}, f32[136,128]{1,0:T(8,128)S(1)}, u32[]{:S(2)}, u32[]{:S(2)}) collective-permute-start(f32[136,128]{1,0:T(8,128)S(1)} %get-tuple-element.25), channel_id=1, source_target_pairs={{0,8},{8,0},{16,24},{24,16},{32,40},{40,32},{48,56},{56,48},{64,72... | collective-permute-start | bytes 208904 | tf_op jit(solution)/shard_map/ppermute | solution.py:500
  19.7 6.8 %collective-permute-start.5 = (f32[136,128]{1,0:T(8,128)S(1)}, f32[136,128]{1,0:T(8,128)S(1)}, u32[]{:S(2)}, u32[]{:S(2)}) collective-permute-start(f32[136,128]{1,0:T(8,128)S(1)} %add.29), channel_id=1, source_target_pairs={{0,192},{8,200},{16,208},{24,216},{32,224},{40,232},{48,240},{56,2... | collective-permute-start | bytes 208904 | tf_op jit(solution)/shard_map/ppermute | solution.py:494
  23.0 6.4 %collective-permute-start.4 = (f32[136,128]{1,0:T(8,128)S(1)}, f32[136,128]{1,0:T(8,128)S(1)}, u32[]{:S(2)}, u32[]{:S(2)}) collective-permute-start(f32[136,128]{1,0:T(8,128)S(1)} %add.29), channel_id=1, source_target_pairs={{0,128},{8,136},{16,144},{24,152},{32,160},{40,168},{48,176},{56,1... | collective-permute-start | bytes 208904 | tf_op jit(solution)/shard_map/ppermute | solution.py:494
  23.3 6.6 %collective-permute-start.3 = (f32[136,128]{1,0:T(8,128)S(1)}, f32[136,128]{1,0:T(8,128)S(1)}, u32[]{:S(2)}, u32[]{:S(2)}) collective-permute-start(f32[136,128]{1,0:T(8,128)S(1)} %add.29), channel_id=1, source_target_pairs={{0,64},{8,72},{16,80},{24,88},{32,96},{40,104},{48,112},{56,120},{... | collective-permute-start | bytes 208904 | tf_op jit(solution)/shard_map/ppermute | solution.py:494
  29.9 5.2 %collective-permute-start.8 = (f32[136,128]{1,0:T(8,128)S(1)}, f32[136,128]{1,0:T(8,128)S(1)}, u32[]{:S(2)}, u32[]{:S(2)}) collective-permute-start(f32[136,128]{1,0:T(8,128)S(1)} %add_add_fusion.1), channel_id=1, source_target_pairs={{0,48},{8,56},{16,0},{24,8},{32,16},{40,24},{48,32},{56,40},{64,11... | collective-permute-start | bytes 208904 | tf_op jit(solution)/shard_map/ppermute | solution.py:494
  31.8 5.8 %collective-permute-start.7 = (f32[136,128]{1,0:T(8,128)S(1)}, f32[136,128]{1,0:T(8,128)S(1)}, u32[]{:S(2)}, u32[]{:S(2)}) collective-permute-start(f32[136,128]{1,0:T(8,128)S(1)} %add_add_fusion.1), channel_id=1, source_target_pairs={{0,32},{8,40},{16,48},{24,56},{32,0},{40,8},{48,16},{56,24},{64,96... | collective-permute-start | bytes 208904 | tf_op jit(solution)/shard_map/ppermute | solution.py:494
  32.6 5.0 %collective-permute-start.6 = (f32[136,128]{1,0:T(8,128)S(1)}, f32[136,128]{1,0:T(8,128)S(1)}, u32[]{:S(2)}, u32[]{:S(2)}) collective-permute-start(f32[136,128]{1,0:T(8,128)S(1)} %add_add_fusion.1), channel_id=1, source_target_pairs={{0,16},{8,24},{16,32},{24,40},{32,48},{40,56},{48,0},{56,8},{64,80... | collective-permute-start | bytes 208904 | tf_op jit(solution)/shard_map/ppermute | solution.py:494
  37.6 1.5 %collective-permute-start.9 = (f32[136,128]{1,0:T(8,128)S(1)}, f32[136,128]{1,0:T(8,128)S(1)}, u32[]{:S(2)}, u32[]{:S(2)}) collective-permute-start(f32[136,128]{1,0:T(8,128)S(1)} %add_add_fusion.mine), channel_id=1, source_target_pairs={{0,8},{8,0},{16,24},{24,16},{32,40},{40,32},{48,56},{56,48},{64,72... | collective-permute-start | bytes 208904 | tf_op jit(solution)/shard_map/ppermute | solution.py:500
  49.3 4.2 %collective-permute-start.10 = (f32[32,128,128]{2,1,0:T(8,128)S(1)}, f32[32,128,128]{2,1,0:T(8,128)S(1)}, u32[]{:S(2)}, u32[]{:S(2)}) collective-permute-start(f32[32,128,128]{2,1,0:T(8,128)S(1)} %get-tuple-element.31), channel_id=1, source_target_pairs={{0,8},{8,0},{16,24},{24,16},{32,40},{40,32},{48,56},{56,48},{64,72... | collective-permute-start | bytes 6291464 | tf_op jit(solution)/shard_map/ppermute | solution.py:500
